TPU v7x, 256 devices: a whole 4x4x8 slice. The times are simulated.
256 devices in a mesh: tm: 128 (over x, z_lo, y, core), mp: 2 (over z_hi).
Axes of the slice: x: 4, y: 4, z: 8 (z_hi: 2, z_lo: 4; z = z_hi * 4 + z_lo), core: 2. Of those that a mesh axis runs over, the one named last changes fastest.
Arguments:
- filterbank: bfloat16 [4, 131072, 80], P(None, 'tm'), may hold values from -6 to 6
- lengths: int32 [4], replicated, may hold values from 16384 to 32768, as said below
- bank_begin: int32 [4, 8192], P(None, 'tm'), may hold values from 0 to 8191, as said below
- memory_in: bfloat16 [4, 8192, 1024], P(None, 'tm', 'mp'), may hold values from -6 to 6
- w_front: bfloat16 [320, 1024], P(None, 'mp'), may hold values from -0.3125 to 0.3125
- gain_attn: float32 [1024], replicated, may hold values from 0.25 to 1.75
- w_query: bfloat16 [1024, 1024], P(None, 'mp'), may hold values from -0.1875 to 0.1875
- w_key: bfloat16 [1024, 1024], P(None, 'mp'), may hold values from -0.1875 to 0.1875
- w_value: bfloat16 [1024, 1024], P(None, 'mp'), may hold values from -0.1875 to 0.1875
- w_out: bfloat16 [1024, 1024], P('mp'), may hold values from -0.1875 to 0.1875
- gain_ffn: float32 [1024], replicated, may hold values from 0.25 to 1.75
- w_up: bfloat16 [1024, 4096], P(None, 'mp'), may hold values from -0.1875 to 0.1875
- w_down: bfloat16 [4096, 1024], P('mp'), may hold values from -0.09375 to 0.09375
Outputs:
- encoded: bfloat16 [4, 32768, 1024], P(None, 'tm', 'mp')
- memory_out: bfloat16 [4, 8192, 1024], P(None, 'tm', 'mp')
Inputs may be any that keep to these rules, and one draw needn't show every extreme that they name: `lengths`: some utterance has all 32768 frames. For segment i: max(0, i - 32) <= bank_begin <= max(0, i - 16); in each utterance some segment has bank_begin = i - 32.
All inputs are finite; a program needn't handle non-finite values.
Results may differ from a plain program's by a relative error of at most 0.012.
Values may be sent and summed in bfloat16 or wider, within the bound.
No kernel may reach another device: no remote copies, remote signals or barrier semaphores. Data moves between devices by JAX's collectives and lax.ppermute only.
A program may use at most 128 MiB of HBM per device.

v0:
```python
import jax
import jax.numpy as jnp
from jax import lax
from jax.experimental import pallas as pl
from jax.experimental.pallas import tpu as pltpu
from jax.sharding import PartitionSpec as P


D = 1024
HALF = 512
SEG = 4
LC = 32
RC = 4
M = 32
NX, NZ, NY, NC = 4, 4, 4, 2
TM = NX * NZ * NY * NC
U = 2
F = 256
S = 64
EXT = 320
QB, KB = 160, 256
KF = 192
epsilon = 1e-05
bf16, f32, i32 = jnp.bfloat16, jnp.float32, jnp.int32
AXES = ("tm", "mp")
GRANTS = {
    "pack": 48,
    "front": 48,
    "own_heads": 48,
    "other_heads": 48,
    "own_hidden": 48,
    "other_hidden": 48,
}


def place(x, z, y, c, m):
    return ((((x % NX) * NZ + z) * NY + y % NY) * NC + c % NC) * 2 + m % 2


def route(step):
    dx, dy, dc, dm = step
    return [
        (place(x, z, y, c, m), place(x + dx, z, y + dy, c + dc, m + dm))
        for x in range(NX)
        for z in range(NZ)
        for y in range(NY)
        for c in range(NC)
        for m in range(2)
    ]


STEPS = {
    ("x", 1): (1, 0, 0, 0),
    ("x", -1): (-1, 0, 0, 0),
    ("y", 1): (0, 1, 0, 0),
    ("y", -1): (0, -1, 0, 0),
    ("c", 1): (0, 0, 1, 0),
    ("m", 1): (0, 0, 0, 1),
}


def moved(array, axis, by=1):
    return lax.ppermute(array, AXES, route(STEPS[axis, by]))


def along_frames(array, by):
    pairs = [
        (t * 2 + m, (t + by) * 2 + m) for t in range(TM) for m in range(2) if 0 <= t + by < TM
    ]
    return lax.ppermute(array, AXES, pairs)


def after(value, *earlier):
    return lax.optimization_barrier((value, *earlier))[0]


def both_ways(array, axis, way):
    back = moved(array, axis, way)
    front = moved(array, axis, -way)
    return back, front


def partners(blocks):
    return [moved(b, "c") for b in blocks]


def each_piece(first, way, where, halves, act):
    x, y, c = where
    far = [(0, 0, 4), (way, 0, 4), (-way, 0, 4)]
    far += [(2, 0, 2), (2, 2, 4)] if halves else [(2, 0, 4)]
    for i, (a2, low, high) in enumerate(far):

        def step(j, carry):
            a1 = jnp.where(j == 0, 0, jnp.where(j == 1, -way, jnp.where(j == 2, way, 2)))
            px = (x + (a1 if first == "x" else a2)) & 3
            py = (y + (a2 if first == "x" else a1)) & 3
            for k in range(2):
                pc = c if k == 0 else 1 - c
                act(i + len(far) * k, j - low, px * 8 + py * 2 + pc)
            return carry

        lax.fori_loop(low, high, step, 0)


def dot(a, b):
    return jnp.dot(a, b, preferred_element_type=f32)


def normed(values, gain):
    center = jnp.sum(values, axis=-1, keepdims=True) * (1.0 / D)
    shifted = values - center
    spread_ = jnp.sum(shifted * shifted, axis=-1, keepdims=True) * (1.0 / D)
    return shifted * lax.rsqrt(spread_ + epsilon) * gain


def gelu(v):
    inner = 0.7978845608028654 * (v + 0.044715 * (v * v * v))
    return 0.5 * v * (1.0 + jnp.tanh(inner))


def pack_kernel(sc, wq, wk, wv, wo, wu, wd, mem, s1, up, down):
    s1[:, :HALF] = wq[...]
    s1[:, HALF : 2 * HALF] = wk[...]
    s1[:, 2 * HALF : 3 * HALF] = wv[...]
    s1[:16, 3 * HALF :] = wo[:, :HALF]
    s1[16:, 3 * HALF :] = wo[:, HALF:]
    up[:, :2048] = wu[...]
    down[...] = wd[...]
    for i in range(4):
        at = slice(2048 + HALF * i, 2048 + HALF * i + HALF)
        up[:, at] = mem[i // 2, 32 * (i % 2) : 32 * (i % 2) + 32, :]


def front_kernel(
    sc, fb, left, right, wf_own, wf_a, wf_b, gain, wq, wk, wv, x_out, n_out, q, k, v, xs, fbs
):
    u = pl.program_id(0)
    h, c = sc[2], sc[5]
    fbs[:LC] = left[0]
    fbs[LC : LC + F] = fb[0]
    fbs[LC + F : LC + F + 16] = right[0]
    fbs[LC + F + 16 :] = jnp.zeros((16, 320), bf16)
    rows = fbs[...]
    pos = sc[3] * F - LC + lax.broadcasted_iota(i32, (EXT, 1), 0)
    valid = pos < sc[u]

    def put(at, width, w):
        part = jnp.where(valid, dot(rows, w[...]), 0.0).astype(bf16)
        xs[:, pl.ds(pl.multiple_of(at, 256), width)] = part

    other = (1 - h) * HALF
    put(h * HALF, HALF, wf_own)
    put(other + c * 256, 256, wf_a)
    put(other + (1 - c) * 256, 256, wf_b)
    x_out[0] = xs[LC : LC + F, :]
    g = gain[...]
    n_out[0, :EXT, :] = normed(xs[...].astype(f32), g).astype(bf16)
    seg = lax.broadcasted_iota(i32, (S, F), 0)
    frame = lax.broadcasted_iota(i32, (S, F), 1)
    pool = jnp.where(frame // SEG == seg, 0.25, 0.0).astype(bf16)
    n_out[0, EXT:, :] = normed(dot(pool, xs[LC : LC + F, :]), g).astype(bf16)
    project(n_out, wq, wk, wv, q, k, v)


def project(n, wq, wk, wv, q, k, v):
    q[0, :F, :] = (dot(n[0, LC : LC + F, :], wq[...]) * 0.125).astype(bf16)
    q[0, F:, :] = (dot(n[0, EXT:, :], wq[...]) * 0.125).astype(bf16)
    k[0] = dot(n[0, :EXT, :], wk[...]).astype(bf16)
    v[0] = dot(n[0, :EXT, :], wv[...]).astype(bf16)


def mask_of(sc, u, b, begins):
    t = sc[3]
    shape = (QB, S)
    r = lax.broadcasted_iota(i32, shape, 0)
    col = lax.broadcasted_iota(i32, shape, 1)
    local = 32 * b + jnp.where(r < 128, r // SEG, r - 128)
    begin = begins[pl.ds(2 * sc[2] + u, 1), :]
    floor = jnp.sum(jnp.where(col == local, begin, 0), axis=-1, keepdims=True)
    r = lax.broadcasted_iota(i32, (QB, 1), 0)
    seg = t * S + 32 * b + jnp.where(r < 128, r // SEG, r - 128)
    k = lax.broadcasted_iota(i32, (QB, KB), 1)
    pos = t * F - LC + 128 * b + k
    bank = t * S - M + 32 * b + k - KF
    low = jnp.maximum(seg * SEG - LC, 0)
    high = jnp.minimum((seg + 1) * SEG + RC, sc[u])
    sees_frame = (k < KF) & (pos >= low) & (pos < high)
    sees_bank = (k >= KF) & (bank >= floor) & (bank <= seg - 1)
    return jnp.where(sees_frame | sees_bank, 0.0, -1e30).astype(f32)


def attend(sc, u, begins, q, k, v, mk, mv, ctx):
    low = lax.broadcasted_iota(i32, (1, 128), 1) < 64

    def block(b, carry):
        mask = mask_of(sc, u, b, begins)
        masks = jnp.concatenate([mask, mask], axis=0)
        at = pl.multiple_of(b * 128, 128)
        few = pl.multiple_of(b * 32, 32)
        fr, sm = pl.ds(at, 128), pl.ds(F + few, 32)
        kr, mr = pl.ds(at, KF), pl.ds(few, 64)
        for p in range(4):
            lanes = slice(128 * p, 128 * p + 128)
            qb = jnp.concatenate([q[0, fr, lanes], q[0, sm, lanes]], axis=0)
            zero = jnp.zeros_like(qb)
            pair = jnp.concatenate([jnp.where(low, qb, zero), jnp.where(low, zero, qb)], axis=0)
            keys = jnp.concatenate([k[0, kr, lanes], mk[mr, lanes]], axis=0)
            values = jnp.concatenate([v[0, kr, lanes], mv[mr, lanes]], axis=0)
            scores = lax.dot_general(
                pair, keys, (((1,), (1,)), ((), ())), preferred_element_type=f32
            )
            weights = jnp.exp(scores + masks)
            total = jnp.sum(weights, axis=-1, keepdims=True)
            shares = (weights * (1.0 / total)).astype(bf16)
            mixed = dot(shares, values)
            part = jnp.where(low, mixed[:QB], mixed[QB:]).astype(bf16)
            ctx[0, fr, lanes] = part[:128]
            ctx[0, sm, lanes] = part[128:]
        return carry

    lax.fori_loop(0, 2, block, 0)


def own_heads_kernel(
    sc, mem_a, mem_b, halo_a, halo_b, begins, gain, wk, wv, q, k, v, ctx, nm, mk, mv, ms
):
    h = sc[2]
    mine = pl.ds(pl.multiple_of(h * HALF, HALF), HALF)
    theirs = pl.ds(pl.multiple_of((1 - h) * HALF, HALF), HALF)
    ms[:M, mine] = halo_a[0]
    ms[M:, mine] = mem_a[0]
    ms[:M, theirs] = halo_b[0]
    ms[M : M + 32, theirs] = mem_b[:, :HALF]
    ms[M + 32 :, theirs] = mem_b[:, HALF:]
    nm[0] = normed(ms[...].astype(f32), gain[...]).astype(bf16)
    mk[...] = dot(nm[0], wk[...]).astype(bf16)
    mv[...] = dot(nm[0], wv[...]).astype(bf16)
    attend(sc, pl.program_id(0), begins, q, k, v, mk, mv, ctx)


def other_heads_kernel(*refs):
    sc, n, nm, begins, ctx_own, x, wo_own, gain = refs[:8]
    parts = refs[8:18]
    hid, nf, memory = refs[18:21]
    wqkv, wo, q, k, v, mk, mv, ctx, sem = refs[21:]
    u = pl.program_id(0)
    where = (sc[4], sc[6], sc[5])

    @pl.when(u == 0)
    def _():
        def fetch(r, j, at):
            rows = pl.ds(pl.multiple_of(at * 32, 32), 32)
            src = parts[r].at[j, :, : 3 * HALF]
            pltpu.make_async_copy(src, wqkv.at[rows], sem.at[0]).start()
            few = pl.ds(pl.multiple_of(at * 16, 16), 16)
            for s in range(2):
                src = parts[r].at[j, 16 * s : 16 * s + 16, 3 * HALF :]
                dst = wo.at[few, HALF * s : HALF * s + HALF]
                pltpu.make_async_copy(src, dst, sem.at[1]).start()

        each_piece("y", -1, where, True, fetch)

    mine = dot(ctx_own[0], wo_own[...]).astype(bf16).astype(f32)

    @pl.when(u == 0)
    def _():
        pltpu.make_async_copy(wqkv, wqkv, sem.at[0]).wait()
        pltpu.make_async_copy(wo, wo, sem.at[1]).wait()

    wk, wv = wqkv.at[:, HALF : 2 * HALF], wqkv.at[:, 2 * HALF :]
    project(n, wqkv.at[:, :HALF], wk, wv, q, k, v)
    mk[...] = dot(nm[0], wk[...]).astype(bf16)
    mv[...] = dot(nm[0], wv[...]).astype(bf16)
    attend(sc, u, begins, q, k, v, mk, mv, ctx)
    theirs = dot(ctx[0], wo[...]).astype(bf16).astype(f32)
    both = mine + theirs
    seg = sc[3] * S + lax.broadcasted_iota(i32, (S, 1), 0)
    memory[0] = jnp.where(seg * SEG < sc[u], both[F:], 0.0).astype(bf16)
    residual = (x[0].astype(f32) + both[:F]).astype(bf16)
    hid[...] = residual
    nf[...] = normed(residual.astype(f32), gain[...]).astype(bf16)


def own_hidden_kernel(nf, wu, wd, out, acc):
    j = pl.program_id(0)

    def some(r, carry):
        rows = pl.ds(pl.multiple_of(r * F, F), F)
        hidden = gelu(dot(nf[rows], wu[...])).astype(bf16)
        part = dot(hidden, wd[...])
        acc[rows] = jnp.where(j == 0, part, acc[rows] + part)
        return carry

    lax.fori_loop(0, U, some, 0)

    @pl.when(j == pl.num_programs(0) - 1)
    def _():
        out[...] = acc[...].astype(bf16)


def other_hidden_kernel(*refs):
    sc, nf, hid, own = refs[:4]
    ups, downs = refs[4:12], refs[12:20]
    out_own, out_other = refs[20:22]
    wu, wd, acc, sem = refs[22:]
    where = (sc[4], sc[6], sc[5])

    def fetch_up(i):
        def fetch(r, j, at):
            rows = pl.ds(pl.multiple_of(at * 32, 32), 32)
            cols = pl.ds(pl.multiple_of(i * HALF, HALF), HALF)
            pltpu.make_async_copy(ups[r].at[j, :, cols], wu.at[i, rows], sem.at[i]).start()

        each_piece("x", 1, where, False, fetch)

    def fetch_down(r, j, at):
        rows = pl.ds(pl.multiple_of(at * 64, 64), 64)
        pltpu.make_async_copy(downs[r].at[j], wd.at[rows], sem.at[4]).start()

    fetch_up(0)
    each_piece("y", -1, where, False, fetch_down)

    def fetch_rest(i, carry):
        fetch_up(i)
        return carry

    lax.fori_loop(1, 4, fetch_rest, 0)

    def step(i, carry):
        pltpu.make_async_copy(wu.at[i], wu.at[i], sem.at[i]).wait()

        @pl.when(i == 0)
        def _():
            pltpu.make_async_copy(wd, wd, sem.at[4]).wait()
            acc[...] = jnp.zeros_like(acc)

        def some(r, carry):
            rows = pl.ds(pl.multiple_of(r * F, F), F)
            hidden = gelu(dot(nf[rows], wu[i])).astype(bf16)
            acc[rows] += dot(hidden, wd[pl.ds(pl.multiple_of(i * HALF, HALF), HALF)])
            return carry

        return lax.fori_loop(0, U, some, carry)

    lax.fori_loop(0, 4, step, 0)
    h = sc[2]
    row = lax.broadcasted_iota(i32, (F, 1), 0)
    for u in range(U):
        valid = sc[3] * F + row < sc[u]
        at = slice(F * u, F * u + F)
        for out, start in ((out_own, h * HALF), (out_other, (1 - h) * HALF)):
            cols = pl.ds(pl.multiple_of(start, HALF), HALF)
            feed = own[at, cols].astype(f32) + acc[at, cols].astype(bf16).astype(f32)
            whole = hid[at, cols].astype(f32) + feed
            out[u] = jnp.where(valid, whole, 0.0).astype(bf16)


def one(shape):
    return pl.BlockSpec((1,) + shape, lambda u, *_: (u,) + (0,) * len(shape))


def all_of(shape):
    return pl.BlockSpec(shape, lambda *_: (0,) * len(shape))


ANY = pl.BlockSpec(memory_space=pl.ANY)


def arrays(*shapes):
    return [jax.ShapeDtypeStruct(s, bf16) for s in shapes]


def kept(*shapes):
    return [pltpu.HBM(s, bf16) for s in shapes]


def stored(array):
    return pltpu.with_memory_space_constraint(array, pltpu.HBM)


def call(kernel, grid, ins, outs, out_shape, scratch, flops, args, scalars=None, name=None):
    spec = pltpu.PrefetchScalarGridSpec(
        num_scalar_prefetch=0 if scalars is None else 1,
        grid=grid,
        in_specs=ins,
        out_specs=outs,
        scratch_shapes=scratch,
    )
    given = list(args) if scalars is None else [scalars, *args]
    return pl.pallas_call(
        kernel,
        grid_spec=spec,
        out_shape=out_shape,
        compiler_params=pltpu.CompilerParams(
            dimension_semantics=("arbitrary",) * len(grid), vmem_limit_bytes=GRANTS[name] << 20
        ),
        cost_estimate=pl.CostEstimate(
            flops=flops, bytes_accessed=8 << 20, transcendentals=1 << 20
        ),
    )(*given)


def cut(array, at, size, dim):
    return lax.dynamic_slice_in_dim(array, at, size, dim)


def joined(own, other, h, dim):
    return jnp.where(
        h == 0,
        jnp.concatenate([own, other], axis=dim),
        jnp.concatenate([other, own], axis=dim),
    )


def body(
    filterbank,
    lengths,
    bank_begin,
    memory_in,
    w_front,
    gain_attn,
    w_query,
    w_key,
    w_value,
    w_out,
    gain_ffn,
    w_up,
    w_down,
):
    t, h = lax.axis_index("tm"), lax.axis_index("mp")
    x_at, y_at, c_at = t // (NZ * NY * NC), (t // NC) % NY, t % NC
    piece = x_at * 8 + y_at * 2 + c_at
    lens = cut(lengths, 2 * h, 2, 0)
    scalars = jnp.concatenate([lens, jnp.stack([h, t, x_at, c_at, y_at, piece]).astype(i32)])

    gain_a, gain_f = gain_attn.reshape(1, D), gain_ffn.reshape(1, D)

    wf_cut = cut(w_front, c_at * 256, 256, 1)
    wf_a = moved(wf_cut, "m")
    wf_b = moved(wf_a, "c")

    def piece_of(rows, width):
        return pl.BlockSpec((rows, width), lambda i, sc: (sc[7], 0))

    weights = [stored(w) for w in (w_query, w_key, w_value, w_out, w_up, w_down)]
    w_query, w_key, w_value, w_out, w_up, w_down = weights
    memory_all = stored(memory_in)
    s1, up, down = call(
        pack_kernel,
        (1,),
        [piece_of(32, HALF)] * 3 + [piece_of(16, D), piece_of(32, 2048), piece_of(64, D)]
        + [pl.BlockSpec((2, S, HALF), lambda i, sc: (1 - sc[2], 0, 0))],
        [all_of((32, 2048)), all_of((32, 4096)), all_of((64, D))],
        arrays((32, 2048), (32, 4096), (64, D)),
        [],
        1 << 20,
        (w_query, w_key, w_value, w_out, w_up, w_down, memory_all),
        after(scalars, wf_cut),
        "pack",
    )
    filterbank = after(filterbank, up)
    s1 = moved(s1, "m")
    up = moved(up, "m")
    down = moved(down, "m")
    back, front = both_ways(s1, "y", -1)
    third = moved(back, "y", -1)
    filled1 = jnp.stack([s1, back, front, third])
    back1, front1 = both_ways(filled1, "x", 1)

    fb = filterbank.reshape(4, F, 320)
    mine = cut(fb, 2 * h, 2, 0)
    left = along_frames(mine[:, F - LC :], 1)
    right = along_frames(mine[:, :16], -1)
    halo_own = along_frames(cut(memory_in, 2 * h, 2, 0)[:, S - M :], 1)

    x, n, q, kk, v = call(
        front_kernel,
        (U,),
        [pl.BlockSpec((1, F, 320), lambda u, sc: (2 * sc[2] + u, 0, 0))]
        + [one((LC, 320)), one((16, 320))]
        + [all_of((320, HALF)), all_of((320, 256)), all_of((320, 256))]
        + [all_of((1, D))]
        + [all_of((D, HALF))] * 3,
        [one((F, D)), one((EXT + S, D))] + [one((EXT, HALF))] * 3,
        kept((U, F, D), (U, EXT + S, D), *[(U, EXT, HALF)] * 3),
        [pltpu.VMEM((EXT, D), bf16), pltpu.VMEM((EXT, 320), bf16)],
        2 * 640 * 1024 * 1536,
        (fb, left, right, w_front, wf_a, wf_b, gain_a, w_query, w_key, w_value),
        scalars,
        "front",
    )
    mem_other, up = up, up[:, :2048]
    late = [mem_other[:, at : at + HALF] for at in (2560, 3584)]
    halo_other = along_frames(jnp.stack(late), 1)
    up_back, up_front = both_ways(up, "x", 1)
    down_back, down_front = both_ways(down, "y", -1)
    ctx, nm = call(
        own_heads_kernel,
        (U,),
        [pl.BlockSpec((1, S, HALF), lambda u, sc: (2 * sc[2] + u, 0, 0))]
        + [pl.BlockSpec((32, D), lambda u, sc: (0, 2 + u))]
        + [one((M, HALF))] * 2
        + [all_of((4, S)), all_of((1, D)), all_of((D, HALF)), all_of((D, HALF))]
        + [one((EXT, HALF))] * 3,
        [one((EXT, HALF)), one((S + M, D))],
        kept((U, EXT, HALF), (U, S + M, D)),
        [pltpu.VMEM((S + M, HALF), bf16)] * 2 + [pltpu.VMEM((S + M, D), bf16)],
        2 << 30,
        (memory_all, mem_other, halo_own, halo_other, bank_begin, gain_a, w_key, w_value, *map(stored, (q, kk, v))),
        scalars,
        "own_heads",
    )
    up_back, down_back = after(up_back, ctx), after(down_back, ctx)
    ups = jnp.stack([up, up_back, up_front, moved(up_back, "x", 1)])
    downs = jnp.stack([down, down_back, down_front, moved(down_back, "y", -1)])
    ups = [ups, *both_ways(ups, "y", -1)]
    downs = [downs, *both_ways(downs, "x", 1)]
    back1, front1, filled1 = after(back1, ctx), after(front1, ctx), after(filled1, ctx)
    blocks1 = [filled1, back1, front1]
    blocks1 += [moved(back1[:2], "x", 1), moved(front1[2:], "x", -1)]
    blocks1 += partners(blocks1)
    hid, nf, memory = call(
        other_heads_kernel,
        (U,),
        [one((EXT + S, D)), one((S + M, D)), all_of((4, S)), one((EXT, HALF)), one((F, D))]
        + [all_of((HALF, D)), all_of((1, D))]
        + [ANY] * 10,
        [pl.BlockSpec((F, D), lambda u, *_: (u, 0))] * 2 + [one((S, D))],
        kept((U * F, D), (U * F, D)) + arrays((U, S, D)),
        [pltpu.VMEM((D, 3 * HALF), bf16), pltpu.VMEM((HALF, D), bf16)]
        + [pltpu.VMEM((1, EXT, HALF), bf16)] * 3
        + [pltpu.VMEM((S + M, HALF), bf16)] * 2
        + [pltpu.VMEM((1, EXT, HALF), bf16), pltpu.SemaphoreType.DMA((2,))],
        6 << 30,
        (stored(n), stored(nm), bank_begin, stored(ctx), stored(x), w_out, gain_f, *blocks1),
        scalars,
        "other_heads",
    )
    ups = [after(w, hid) for w in ups]
    downs = [after(w, hid) for w in downs]
    up_far = moved(ups[1], "y", -1)
    down_far = moved(downs[1], "x", 1)
    up_partners, down_partners = partners(ups), partners(downs)
    memory_other = moved(cut(memory, (1 - h) * HALF, HALF, 2), "m")
    rows = U * F
    own = call(
        own_hidden_kernel,
        (4,),
        [
            all_of((rows, D)),
            pl.BlockSpec((D, HALF), lambda j: (0, j)),
            pl.BlockSpec((HALF, D), lambda j: (j, 0)),
        ],
        all_of((rows, D)),
        kept((rows, D))[0],
        [pltpu.VMEM((rows, D), f32)],
        4 << 30,
        (stored(nf), w_up, w_down),
        None,
        "own_hidden",
    )
    up_far, down_far = after(up_far, own), after(down_far, own)
    ups += [up_far, *up_partners, *partners([up_far])]
    downs += [down_far, *down_partners, *partners([down_far])]
    memory_other, hid = lax.optimization_barrier((memory_other, hid))
    out_own, out_other = call(
        other_hidden_kernel,
        (1,),
        [all_of((rows, D))] * 3 + [ANY] * 16,
        [all_of((U, F, HALF))] * 2,
        arrays((U, F, HALF), (U, F, HALF)),
        [
            pltpu.VMEM((4, D, HALF), bf16),
            pltpu.VMEM((2048, D), bf16),
            pltpu.VMEM((rows, D), f32),
            pltpu.SemaphoreType.DMA((5,)),
        ],
        4 << 30,
        (stored(nf), stored(hid), stored(own), *ups, *downs),
        scalars,
        "other_hidden",
    )
    memory_out = joined(cut(memory, h * HALF, HALF, 2), memory_other, h, 0)
    encoded = joined(out_own, moved(out_other, "m"), h, 0)
    return encoded, memory_out


def solution(mesh):
    in_specs = (
        P(None, "tm", None),
        P(),
        P(None, "tm"),
        P(None, "tm", "mp"),
        P(None, "mp"),
        P(),
        P(None, "mp"),
        P(None, "mp"),
        P(None, "mp"),
        P("mp", None),
        P(),
        P(None, "mp"),
        P("mp", None),
    )
    out_specs = (P(None, "tm", "mp"), P(None, "tm", "mp"))

    return jax.shard_map(body, mesh=mesh, in_specs=in_specs, out_specs=out_specs, check_vma=False)
```

profile of v0, /device:TPU:1, one launch (start us, length us, event | category | flops | bytes accessed | tf_op | source)
XLA Modules:
  0.0 188.3 jit_solution(487616721656424023)
XLA Ops:
  0.7 0.9 constant_dynamic-slice_fusion.5
  1.6 0.7 dynamic_slice.18
  2.4 0.1 concatenate.15.sc.refs_0_
  2.4 1.7 shard_map.140
  4.2 7.8 %collective-permute-start.7 = (bf16[32,2048]{1,0:T(8,128)(2,1)S(1)}, bf16[32,2048]{1,0:T(8,128)(2,1)S(1)}, u32[]{:S(2)}, u32[]{:S(2)}) collective-permute-start(bf16[32,2048]{1,0:T(8,128)(2,1)S(1)} %get-tuple-element.44), channel_id=1, source_target_pairs={{0,1},{1,0},{2,3},{3,2},{4,5},{5,4},{6,7},{7,6},{8,9},{9,8},{10,11... | collective-permute-start | bytes 393224 | tf_op jit(solution)/shard_map/ppermute | solution.py:63
  12.0 0.1 collective-permute-start.2
  12.1 5.3 %collective-permute-start.4 = (bf16[32,4096]{1,0:T(8,128)(2,1)S(1)}, bf16[32,4096]{1,0:T(8,128)(2,1)S(1)}, u32[]{:S(2)}, u32[]{:S(2)}) collective-permute-start(bf16[32,4096]{1,0:T(8,128)(2,1)S(1)} %get-tuple-element.35), channel_id=1, source_target_pairs={{0,1},{1,0},{2,3},{3,2},{4,5},{5,4},{6,7},{7,6},{8,9},{9,8},{10,11... | collective-permute-start | bytes 786440 | tf_op jit(solution)/shard_map/ppermute | solution.py:63
  17.3 0.7 copy.16
  18.0 0.7 reshape.13.fb
  18.7 4.6 %collective-permute-start = (bf16[2,32,320]{2,1,0:T(8,128)(2,1)S(1)}, bf16[2,32,320]{2,1,0:T(8,128)(2,1)S(1)}, u32[]{:S(2)}, u32[]{:S(2)}) collective-permute-start(bf16[2,32,320]{2,1,0:T(8,128)(2,1)S(1)} %constant_dynamic-slice_fusion), channel_id=1, source_target_pairs={{0,2},{1,3},{2,4},{3,5},{4,6},{5,7},{6,8},{7,9},{8,10},{9,11},{10,... | collective-permute-start | bytes 122888 | tf_op jit(solution)/shard_map/ppermute | solution.py:70
  23.4 1.9 %collective-permute-start.8 = (bf16[32,2048]{1,0:T(8,128)(2,1)S(1)}, bf16[32,2048]{1,0:T(8,128)(2,1)S(1)}, u32[]{:S(2)}, u32[]{:S(2)}) collective-permute-start(bf16[32,2048]{1,0:T(8,128)(2,1)S(1)} %collective-permute-done.7), channel_id=1, source_target_pairs={{0,12},{1,13},{2,14},{3,15},{4,0},{5,1},{6,2},{7,3},{8,4},{9,5},{1... | collective-permute-start | bytes 393224 | tf_op jit(solution)/shard_map/ppermute | solution.py:63
  25.3 1.9 %collective-permute-start.1 = (bf16[2,16,320]{2,1,0:T(8,128)(2,1)S(1)}, bf16[2,16,320]{2,1,0:T(8,128)(2,1)S(1)}, u32[]{:S(2)}, u32[]{:S(2)}) collective-permute-start(bf16[2,16,320]{2,1,0:T(8,128)(2,1)S(1)} %constant_dynamic-slice_fusion.4), channel_id=1, source_target_pairs={{2,0},{3,1},{4,2},{5,3},{6,4},{7,5},{8,6},{9,7},{10,8},{11,9},{12,... | collective-permute-start | bytes 61448 | tf_op jit(solution)/shard_map/ppermute | solution.py:70
  27.2 0.9 constant_dynamic-slice_fusion.3
  28.0 3.7 %collective-permute-done.4.mem_b = bf16[32,4096]{1,0:T(8,128)(2,1)S(1)} collective-permute-done((bf16[32,4096]{1,0:T(8,128)(2,1)S(1)}, bf16[32,4096]{1,0:T(8,128)(2,1)S(1)}, u32[]{:S(2)}, u32[]{:S(2)}) %collective-permute-start.4) | collective-permute-done | bytes 262176 | tf_op jit(solution)/shard_map/ppermute | solution.py:63
  31.7 1.3 collective-permute-start.9
  33.0 4.5 %collective-permute-start.10 = (bf16[32,2048]{1,0:T(8,128)(2,1)S(1)}, bf16[32,2048]{1,0:T(8,128)(2,1)S(1)}, u32[]{:S(2)}, u32[]{:S(2)}) collective-permute-start(bf16[32,2048]{1,0:T(8,128)(2,1)S(1)} %collective-permute-done.8), channel_id=1, source_target_pairs={{0,12},{1,13},{2,14},{3,15},{4,0},{5,1},{6,2},{7,3},{8,4},{9,5},{1... | collective-permute-start | bytes 393224 | tf_op jit(solution)/shard_map/ppermute | solution.py:63
  37.6 5.9 %collective-permute-start.31 = (bf16[64,1024]{1,0:T(8,128)(2,1)S(1)}, bf16[64,1024]{1,0:T(8,128)(2,1)S(1)}, u32[]{:S(2)}, u32[]{:S(2)}) collective-permute-start(bf16[64,1024]{1,0:T(8,128)(2,1)S(1)} %get-tuple-element.57), channel_id=1, source_target_pairs={{0,1},{1,0},{2,3},{3,2},{4,5},{5,4},{6,7},{7,6},{8,9},{9,8},{10,11... | collective-permute-start | bytes 393224 | tf_op jit(solution)/shard_map/ppermute | solution.py:63
  43.5 2.8 %collective-permute-start.3 = (bf16[320,256]{1,0:T(8,128)(2,1)S(1)}, bf16[320,256]{1,0:T(8,128)(2,1)S(1)}, u32[]{:S(2)}, u32[]{:S(2)}) collective-permute-start(bf16[320,256]{1,0:T(8,128)(2,1)S(1)} %collective-permute-done.2.wf_a), channel_id=1, source_target_pairs={{0,2},{1,3},{2,0},{3,1},{4,6},{5,7},{6,4},{7,5},{8,10},{9,11},{10,... | collective-permute-start | bytes 491528 | tf_op jit(solution)/shard_map/ppermute | solution.py:63
  46.4 0.1 pad_maximum_fusion.refs_8_
  46.4 2.6 %collective-permute-start.12 = (bf16[4,32,2048]{2,1,0:T(8,128)(2,1)S(1)}, bf16[4,32,2048]{2,1,0:T(8,128)(2,1)S(1)}, u32[]{:S(2)}, u32[]{:S(2)}) collective-permute-start(bf16[4,32,2048]{2,1,0:T(8,128)(2,1)S(1)} %pad_maximum_fusion.refs_8_), channel_id=1, source_target_pairs={{0,192},{1,193},{2,194},{3,195},{4,196},{5,197},{6,198},{7,199},{8... | collective-permute-start | bytes 1572872 | tf_op jit(solution)/shard_map/ppermute | solution.py:63
  49.0 0.1 collective-permute-start.11
  49.1 1.9 %collective-permute-start.5 = (bf16[2,32,512]{2,1,0:T(8,128)(2,1)S(1)}, bf16[2,32,512]{2,1,0:T(8,128)(2,1)S(1)}, u32[]{:S(2)}, u32[]{:S(2)}) collective-permute-start(bf16[2,32,512]{2,1,0:T(8,128)(2,1)S(1)} %constant_dynamic-slice_fusion.3), channel_id=1, source_target_pairs={{0,2},{1,3},{2,4},{3,5},{4,6},{5,7},{6,8},{7,9},{8,10},{9,11},{10,... | collective-permute-start | bytes 196616 | tf_op jit(solution)/shard_map/ppermute | solution.py:70
  51.1 3.6 %collective-permute-start.32 = (bf16[64,1024]{1,0:T(8,128)(2,1)S(1)}, bf16[64,1024]{1,0:T(8,128)(2,1)S(1)}, u32[]{:S(2)}, u32[]{:S(2)}) collective-permute-start(bf16[64,1024]{1,0:T(8,128)(2,1)S(1)} %collective-permute-done.31), channel_id=1, source_target_pairs={{0,12},{1,13},{2,14},{3,15},{4,0},{5,1},{6,2},{7,3},{8,4},{9,5},{1... | collective-permute-start | bytes 393224 | tf_op jit(solution)/shard_map/ppermute | solution.py:63
  54.6 1.9 %collective-permute-start.6 = (bf16[2,32,512]{2,1,0:T(8,128)(2,1)S(1)}, bf16[2,32,512]{2,1,0:T(8,128)(2,1)S(1)}, u32[]{:S(2)}, u32[]{:S(2)}) collective-permute-start(bf16[2,32,512]{2,1,0:T(8,128)(2,1)S(1)} %pad_maximum_fusion.3), channel_id=1, source_target_pairs={{0,2},{1,3},{2,4},{3,5},{4,6},{5,7},{6,8},{7,9},{8,10},{9,11},{10,... | collective-permute-start | bytes 196616 | tf_op jit(solution)/shard_map/ppermute | solution.py:70
  56.6 7.9 %shard_map.141 = (bf16[2,256,1024]{2,1,0:T(8,128)(2,1)}, bf16[2,384,1024]{2,1,0:T(8,128)(2,1)}, bf16[2,320,512]{2,1,0:T(8,128)(2,1)}, bf16[2,320,512]{2,1,0:T(8,128)(2,1)}, bf16[2,320,512]{2,1,0:T(8,128)(2,1)}) custom-call(s32[8]{0:T(128)S(1)} %concatenate.15.sc.refs_0_, bf16[4,256,320]{2,1,0:T(8,128)(2,1)S(1)} %reshape.13.fb, ...), custom_call_target="tpu_custom_call" | custom-call | flops 2013265920 | bytes 8388608 | tf_op jit(solution)/shard_map/pallas_call | solution.py:390
  64.6 1.0 collective-permute-start.21
  65.6 7.4 %shard_map.142 = (bf16[2,320,512]{2,1,0:T(8,128)(2,1)}, bf16[2,96,1024]{2,1,0:T(8,128)(2,1)}) custom-call(s32[8]{0:T(128)S(1)} %concatenate.15.sc.refs_0_, bf16[4,64,512]{2,1,0:T(8,128)(2,1)} %mem_a.1, bf16[32,4096]{1,0:T(8,128)(2,1)S(1)} %collective-permute-done.4.mem_b, bf16[2,32,512]{2,1,0:T(8,128)(2,1)S(1)} %collective-permute-done.5.halo_a, ...), custom_call_target="tpu_custom_call" | custom-call | flops 2147483648 | bytes 8388608 | tf_op jit(solution)/shard_map/pallas_call | solution.py:390
  73.0 2.3 %collective-permute-start.22 = (bf16[32,2048]{1,0:T(8,128)(2,1)S(1)}, bf16[32,2048]{1,0:T(8,128)(2,1)S(1)}, u32[]{:S(2)}, u32[]{:S(2)}) collective-permute-start(bf16[32,2048]{1,0:T(8,128)(2,1)S(1)} %get-tuple-element.69), channel_id=1, source_target_pairs={{0,192},{1,193},{2,194},{3,195},{4,196},{5,197},{6,198},{7,199},{8... | collective-permute-start | bytes 393224 | tf_op jit(solution)/shard_map/ppermute | solution.py:63
  75.3 2.4 %collective-permute-start.34 = (bf16[64,1024]{1,0:T(8,128)(2,1)S(1)}, bf16[64,1024]{1,0:T(8,128)(2,1)S(1)}, u32[]{:S(2)}, u32[]{:S(2)}) collective-permute-start(bf16[64,1024]{1,0:T(8,128)(2,1)S(1)} %collective-permute-done.32), channel_id=1, source_target_pairs={{0,12},{1,13},{2,14},{3,15},{4,0},{5,1},{6,2},{7,3},{8,4},{9,5},{1... | collective-permute-start | bytes 393224 | tf_op jit(solution)/shard_map/ppermute | solution.py:63
  77.8 2.8 %collective-permute-start.14 = (bf16[2,32,2048]{2,1,0:T(8,128)(2,1)S(1)}, bf16[2,32,2048]{2,1,0:T(8,128)(2,1)S(1)}, u32[]{:S(2)}, u32[]{:S(2)}) collective-permute-start(bf16[2,32,2048]{2,1,0:T(8,128)(2,1)S(1)} %slice.30), channel_id=1, source_target_pairs={{0,192},{1,193},{2,194},{3,195},{4,196},{5,197},{6,198},{7,199},{8... | collective-permute-start | bytes 786440 | tf_op jit(solution)/shard_map/ppermute | solution.py:63
  80.5 0.1 collective-permute-start.13
  80.6 2.0 %collective-permute-start.15 = (bf16[4,32,2048]{2,1,0:T(8,128)(2,1)S(1)}, bf16[4,32,2048]{2,1,0:T(8,128)(2,1)S(1)}, u32[]{:S(2)}, u32[]{:S(2)}) collective-permute-start(bf16[4,32,2048]{2,1,0:T(8,128)(2,1)S(1)} %pad_maximum_fusion.refs_8_), channel_id=1, source_target_pairs={{0,2},{1,3},{2,0},{3,1},{4,6},{5,7},{6,4},{7,5},{8,10},{9,11},{10,... | collective-permute-start | bytes 1572872 | tf_op jit(solution)/shard_map/ppermute | solution.py:63
  82.6 0.1 collective-permute-start.17
  82.8 2.8 %collective-permute-start.16 = (bf16[4,32,2048]{2,1,0:T(8,128)(2,1)S(1)}, bf16[4,32,2048]{2,1,0:T(8,128)(2,1)S(1)}, u32[]{:S(2)}, u32[]{:S(2)}) collective-permute-start(bf16[4,32,2048]{2,1,0:T(8,128)(2,1)S(1)} %collective-permute-done.11.refs_9_), channel_id=1, source_target_pairs={{0,2},{1,3},{2,0},{3,1},{4,6},{5,7},{6,4},{7,5},{8,10},{9,11},{10,... | collective-permute-start | bytes 1572872 | tf_op jit(solution)/shard_map/ppermute | solution.py:63
  85.6 1.5 collective-permute-start.19
  87.0 1.4 collective-permute-done.13.refs_11_
  88.4 2.5 %collective-permute-start.18 = (bf16[2,32,2048]{2,1,0:T(8,128)(2,1)S(1)}, bf16[2,32,2048]{2,1,0:T(8,128)(2,1)S(1)}, u32[]{:S(2)}, u32[]{:S(2)}) collective-permute-start(bf16[2,32,2048]{2,1,0:T(8,128)(2,1)S(1)} %collective-permute-done.13.refs_11_), channel_id=1, source_target_pairs={{0,2},{1,3},{2,0},{3,1},{4,6},{5,7},{6,4},{7,5},{8,10},{9,11},{10,... | collective-permute-start | bytes 786440 | tf_op jit(solution)/shard_map/ppermute | solution.py:63
  90.9 0.1 pad_maximum_fusion.1.refs_4_
  91.0 0.1 collective-permute-start.35
  91.1 2.7 %collective-permute-start.36 = (bf16[4,64,1024]{2,1,0:T(8,128)(2,1)S(1)}, bf16[4,64,1024]{2,1,0:T(8,128)(2,1)}, u32[]{:S(2)}, u32[]{:S(2)}) collective-permute-start(bf16[4,64,1024]{2,1,0:T(8,128)(2,1)S(1)} %pad_maximum_fusion.2.refs_12_), channel_id=1, source_target_pairs={{0,192},{1,193},{2,194},{3,195},{4,196},{5,197},{6,198},{7,199},{8... | collective-permute-start | bytes 1572872 | tf_op jit(solution)/shard_map/ppermute | solution.py:63
  93.8 0.3 collective-permute-start.24
  94.1 1.2 collective-permute-start.25
  95.3 14.5 %shard_map.143 = (bf16[512,1024]{1,0:T(8,128)(2,1)}, bf16[512,1024]{1,0:T(8,128)(2,1)}, bf16[2,64,1024]{2,1,0:T(8,128)(2,1)S(1)}) custom-call(s32[8]{0:T(128)S(1)} %concatenate.15.sc.refs_0_, bf16[2,384,1024]{2,1,0:T(8,128)(2,1)} %get-tuple-element.37.refs_1_, bf16[2,96,1024]{2,1,0:T(8,128)(2,1)} %get-tuple-element.41.refs_2_, s32[4,64]{1,0:T(4,128)S(1)} %copy-done.3, ...), custom_call_target="tpu_custom_call" | custom-call | flops 6442450944 | bytes 8388608 | tf_op jit(solution)/shard_map/pallas_call | solution.py:390
  109.8 0.1 collective-permute-start.37
  109.9 1.6 collective-permute-start.26
  111.5 1.4 collective-permute-start.40
  112.8 0.5 collective-permute-start.38
  113.4 10.4 %collective-permute-done.37.refs_15_ = bf16[4,64,1024]{2,1,0:T(8,128)(2,1)} collective-permute-done((bf16[4,64,1024]{2,1,0:T(8,128)(2,1)}, bf16[4,64,1024]{2,1,0:T(8,128)(2,1)}, u32[]{:S(2)}, u32[]{:S(2)}) %collective-permute-start.37) | collective-permute-done | bytes 524320 | tf_op jit(solution)/shard_map/ppermute | solution.py:63
  123.7 3.5 %collective-permute-start.20 = (bf16[2,64,512]{2,1,0:T(8,128)(2,1)S(1)}, bf16[2,64,512]{2,1,0:T(8,128)(2,1)S(1)}, u32[]{:S(2)}, u32[]{:S(2)}) collective-permute-start(bf16[2,64,512]{2,1,0:T(8,128)(2,1)S(1)} %get-tuple-element.67), channel_id=1, source_target_pairs={{0,1},{1,0},{2,3},{3,2},{4,5},{5,4},{6,7},{7,6},{8,9},{9,8},{10,11... | collective-permute-start | bytes 393224 | tf_op jit(solution)/shard_map/ppermute | solution.py:63
  127.2 10.1 %shard_map.144.refs_3_ = bf16[512,1024]{1,0:T(8,128)(2,1)} custom-call(bf16[512,1024]{1,0:T(8,128)(2,1)} %get-tuple-element.48.nf.refs_1_, bf16[1024,2048]{1,0:T(8,128)(2,1)} %wu.3, bf16[2048,1024]{1,0:T(8,128)(2,1)} %wd.3), custom_call_target="tpu_custom_call" | custom-call | flops 4294967296 | bytes 8388608 | tf_op jit(solution)/shard_map/pallas_call | solution.py:390
  137.3 2.3 %collective-permute-start.28 = (bf16[4,32,2048]{2,1,0:T(8,128)(2,1)S(1)}, bf16[4,32,2048]{2,1,0:T(8,128)(2,1)S(1)}, u32[]{:S(2)}, u32[]{:S(2)}) collective-permute-start(bf16[4,32,2048]{2,1,0:T(8,128)(2,1)S(1)} %collective-permute-done.24.refs_5_), channel_id=1, source_target_pairs={{0,2},{1,3},{2,0},{3,1},{4,6},{5,7},{6,4},{7,5},{8,10},{9,11},{10,... | collective-permute-start | bytes 1572872 | tf_op jit(solution)/shard_map/ppermute | solution.py:63
  139.6 0.1 collective-permute-start.29
  139.7 0.4 collective-permute-start.27
  140.1 0.1 collective-permute-start.41
  140.2 0.4 collective-permute-start.30
  140.6 1.2 collective-permute-done.29.refs_10_
  141.9 0.7 collective-permute-done.27.refs_8_
  142.6 0.7 collective-permute-done.41.refs_19_
  143.3 0.7 collective-permute-done.30.refs_11_
  144.2 13.9 %shard_map.145 = (bf16[2,256,512]{2,1,0:T(8,128)(2,1)S(1)}, bf16[2,256,512]{2,1,0:T(8,128)(2,1)}) custom-call(s32[8]{0:T(128)S(1)} %concatenate.15.sc.refs_0_, bf16[512,1024]{1,0:T(8,128)(2,1)} %get-tuple-element.48.nf.refs_1_, bf16[512,1024]{1,0:T(8,128)(2,1)} %get-tuple-element.51.refs_2_, bf16[512,1024]{1,0:T(8,128)(2,1)} %shard_map.144.refs_3_, ...), custom_call_target="tpu_custom_call" | custom-call | flops 4294967296 | bytes 8388608 | tf_op jit(solution)/shard_map/pallas_call | solution.py:390
  158.1 1.9 %collective-permute-start.42 = (bf16[2,256,512]{2,1,0:T(8,128)(2,1)}, bf16[2,256,512]{2,1,0:T(8,128)(2,1)S(1)}, u32[]{:S(2)}, u32[]{:S(2)}) collective-permute-start(bf16[2,256,512]{2,1,0:T(8,128)(2,1)} %get-tuple-element.64), channel_id=1, source_target_pairs={{0,1},{1,0},{2,3},{3,2},{4,5},{5,4},{6,7},{7,6},{8,9},{9,8},{10,11... | collective-permute-start | bytes 1572872 | tf_op jit(solution)/shard_map/ppermute | solution.py:63
  160.1 0.7 maximum_select_fusion.1
  160.8 26.4 %collective-permute-done.42 = bf16[2,256,512]{2,1,0:T(8,128)(2,1)S(1)} collective-permute-done((bf16[2,256,512]{2,1,0:T(8,128)(2,1)}, bf16[2,256,512]{2,1,0:T(8,128)(2,1)S(1)}, u32[]{:S(2)}, u32[]{:S(2)}) %collective-permute-start.42) | collective-permute-done | bytes 524320 | tf_op jit(solution)/shard_map/ppermute | solution.py:63
  187.2 1.1 maximum_select_fusion
  (59 shorter events, 0.4 us)
Async XLA Ops:
  2.4 14.9 %copy-start.4 = (bf16[4,1024,80]{1,2,0:T(8,128)(2,1)S(1)}, bf16[4,1024,80]{1,2,0:T(8,128)(2,1)}, u32[]{:S(2)}) copy-start(bf16[4,1024,80]{1,2,0:T(8,128)(2,1)} %param.13) | copy-start | bytes 1966084
  4.1 52.4 %copy-start = (bf16[320,512]{1,0:T(8,128)(2,1)S(1)}, bf16[320,512]{1,0:T(8,128)(2,1)}, u32[]{:S(2)}) copy-start(bf16[320,512]{1,0:T(8,128)(2,1)} %wf_own.1) | copy-start | bytes 983044
  4.1 52.4 %copy-start.1 = (f32[1024]{0:T(1024)S(1)}, f32[1024]{0:T(1024)}, u32[]{:S(2)}) copy-start(f32[1024]{0:T(1024)} %param.18) | copy-start | bytes 12292
  4.2 19.2 %collective-permute-start.7 = (bf16[32,2048]{1,0:T(8,128)(2,1)S(1)}, bf16[32,2048]{1,0:T(8,128)(2,1)S(1)}, u32[]{:S(2)}, u32[]{:S(2)}) collective-permute-start(bf16[32,2048]{1,0:T(8,128)(2,1)S(1)} %get-tuple-element.44), channel_id=1, source_target_pairs={{0,1},{1,0},{2,3},{3,2},{4,5},{5,4},{6,7},{7,6},{8,9},{9,8},{10,11... | collective-permute-start | bytes 393224 | tf_op jit(solution)/shard_map/ppermute | solution.py:63
  12.0 25.6 %collective-permute-start.2 = (bf16[320,256]{1,0:T(8,128)(2,1)S(1)}, bf16[320,256]{1,0:T(8,128)(2,1)S(1)}, u32[]{:S(2)}, u32[]{:S(2)}) collective-permute-start(bf16[320,256]{1,0:T(8,128)(2,1)S(1)} %constant_dynamic-slice_fusion.5), channel_id=1, source_target_pairs={{0,1},{1,0},{2,3},{3,2},{4,5},{5,4},{6,7},{7,6},{8,9},{9,8},{10,11... | collective-permute-start | bytes 491528 | tf_op jit(solution)/shard_map/ppermute | solution.py:63
  12.1 19.7 %collective-permute-start.4 = (bf16[32,4096]{1,0:T(8,128)(2,1)S(1)}, bf16[32,4096]{1,0:T(8,128)(2,1)S(1)}, u32[]{:S(2)}, u32[]{:S(2)}) collective-permute-start(bf16[32,4096]{1,0:T(8,128)(2,1)S(1)} %get-tuple-element.35), channel_id=1, source_target_pairs={{0,1},{1,0},{2,3},{3,2},{4,5},{5,4},{6,7},{7,6},{8,9},{9,8},{10,11... | collective-permute-start | bytes 786440 | tf_op jit(solution)/shard_map/ppermute | solution.py:63
  18.7 30.4 %collective-permute-start = (bf16[2,32,320]{2,1,0:T(8,128)(2,1)S(1)}, bf16[2,32,320]{2,1,0:T(8,128)(2,1)S(1)}, u32[]{:S(2)}, u32[]{:S(2)}) collective-permute-start(bf16[2,32,320]{2,1,0:T(8,128)(2,1)S(1)} %constant_dynamic-slice_fusion), channel_id=1, source_target_pairs={{0,2},{1,3},{2,4},{3,5},{4,6},{5,7},{6,8},{7,9},{8,10},{9,11},{10,... | collective-permute-start | bytes 122888 | tf_op jit(solution)/shard_map/ppermute | solution.py:70
  23.4 9.7 %collective-permute-start.8 = (bf16[32,2048]{1,0:T(8,128)(2,1)S(1)}, bf16[32,2048]{1,0:T(8,128)(2,1)S(1)}, u32[]{:S(2)}, u32[]{:S(2)}) collective-permute-start(bf16[32,2048]{1,0:T(8,128)(2,1)S(1)} %collective-permute-done.7), channel_id=1, source_target_pairs={{0,12},{1,13},{2,14},{3,15},{4,0},{5,1},{6,2},{7,3},{8,4},{9,5},{1... | collective-permute-start | bytes 393224 | tf_op jit(solution)/shard_map/ppermute | solution.py:63
  25.3 23.7 %collective-permute-start.1 = (bf16[2,16,320]{2,1,0:T(8,128)(2,1)S(1)}, bf16[2,16,320]{2,1,0:T(8,128)(2,1)S(1)}, u32[]{:S(2)}, u32[]{:S(2)}) collective-permute-start(bf16[2,16,320]{2,1,0:T(8,128)(2,1)S(1)} %constant_dynamic-slice_fusion.4), channel_id=1, source_target_pairs={{2,0},{3,1},{4,2},{5,3},{6,4},{7,5},{8,6},{9,7},{10,8},{11,9},{12,... | collective-permute-start | bytes 61448 | tf_op jit(solution)/shard_map/ppermute | solution.py:70
  31.7 11.8 %collective-permute-start.9 = (bf16[32,2048]{1,0:T(8,128)(2,1)S(1)}, bf16[32,2048]{1,0:T(8,128)(2,1)S(1)}, u32[]{:S(2)}, u32[]{:S(2)}) collective-permute-start(bf16[32,2048]{1,0:T(8,128)(2,1)S(1)} %collective-permute-done.7), channel_id=1, source_target_pairs={{0,4},{1,5},{2,6},{3,7},{4,8},{5,9},{6,10},{7,11},{8,12},{9,13},{1... | collective-permute-start | bytes 393224 | tf_op jit(solution)/shard_map/ppermute | solution.py:63
  33.0 13.3 %collective-permute-start.10 = (bf16[32,2048]{1,0:T(8,128)(2,1)S(1)}, bf16[32,2048]{1,0:T(8,128)(2,1)S(1)}, u32[]{:S(2)}, u32[]{:S(2)}) collective-permute-start(bf16[32,2048]{1,0:T(8,128)(2,1)S(1)} %collective-permute-done.8), channel_id=1, source_target_pairs={{0,12},{1,13},{2,14},{3,15},{4,0},{5,1},{6,2},{7,3},{8,4},{9,5},{1... | collective-permute-start | bytes 393224 | tf_op jit(solution)/shard_map/ppermute | solution.py:63
  37.6 13.5 %collective-permute-start.31 = (bf16[64,1024]{1,0:T(8,128)(2,1)S(1)}, bf16[64,1024]{1,0:T(8,128)(2,1)S(1)}, u32[]{:S(2)}, u32[]{:S(2)}) collective-permute-start(bf16[64,1024]{1,0:T(8,128)(2,1)S(1)} %get-tuple-element.57), channel_id=1, source_target_pairs={{0,1},{1,0},{2,3},{3,2},{4,5},{5,4},{6,7},{7,6},{8,9},{9,8},{10,11... | collective-permute-start | bytes 393224 | tf_op jit(solution)/shard_map/ppermute | solution.py:63
  43.5 11.1 %collective-permute-start.3 = (bf16[320,256]{1,0:T(8,128)(2,1)S(1)}, bf16[320,256]{1,0:T(8,128)(2,1)S(1)}, u32[]{:S(2)}, u32[]{:S(2)}) collective-permute-start(bf16[320,256]{1,0:T(8,128)(2,1)S(1)} %collective-permute-done.2.wf_a), channel_id=1, source_target_pairs={{0,2},{1,3},{2,0},{3,1},{4,6},{5,7},{6,4},{7,5},{8,10},{9,11},{10,... | collective-permute-start | bytes 491528 | tf_op jit(solution)/shard_map/ppermute | solution.py:63
  46.4 19.2 %copy-start.3 = (s32[4,64]{1,0:T(4,128)S(1)}, s32[4,64]{1,0:T(4,128)}, u32[]{:S(2)}) copy-start(s32[4,64]{1,0:T(4,128)} %refs_3_.1) | copy-start | bytes 3076
  46.4 31.3 %collective-permute-start.12 = (bf16[4,32,2048]{2,1,0:T(8,128)(2,1)S(1)}, bf16[4,32,2048]{2,1,0:T(8,128)(2,1)S(1)}, u32[]{:S(2)}, u32[]{:S(2)}) collective-permute-start(bf16[4,32,2048]{2,1,0:T(8,128)(2,1)S(1)} %pad_maximum_fusion.refs_8_), channel_id=1, source_target_pairs={{0,192},{1,193},{2,194},{3,195},{4,196},{5,197},{6,198},{7,199},{8... | collective-permute-start | bytes 1572872 | tf_op jit(solution)/shard_map/ppermute | solution.py:63
  49.0 28.8 %collective-permute-start.11 = (bf16[4,32,2048]{2,1,0:T(8,128)(2,1)S(1)}, bf16[4,32,2048]{2,1,0:T(8,128)(2,1)S(1)}, u32[]{:S(2)}, u32[]{:S(2)}) collective-permute-start(bf16[4,32,2048]{2,1,0:T(8,128)(2,1)S(1)} %pad_maximum_fusion.refs_8_), channel_id=1, source_target_pairs={{0,64},{1,65},{2,66},{3,67},{4,68},{5,69},{6,70},{7,71},{8,72},{9,... | collective-permute-start | bytes 1572872 | tf_op jit(solution)/shard_map/ppermute | solution.py:63
  49.1 15.4 %collective-permute-start.5 = (bf16[2,32,512]{2,1,0:T(8,128)(2,1)S(1)}, bf16[2,32,512]{2,1,0:T(8,128)(2,1)S(1)}, u32[]{:S(2)}, u32[]{:S(2)}) collective-permute-start(bf16[2,32,512]{2,1,0:T(8,128)(2,1)S(1)} %constant_dynamic-slice_fusion.3), channel_id=1, source_target_pairs={{0,2},{1,3},{2,4},{3,5},{4,6},{5,7},{6,8},{7,9},{8,10},{9,11},{10,... | collective-permute-start | bytes 196616 | tf_op jit(solution)/shard_map/ppermute | solution.py:70
  51.1 21.9 %collective-permute-start.32 = (bf16[64,1024]{1,0:T(8,128)(2,1)S(1)}, bf16[64,1024]{1,0:T(8,128)(2,1)S(1)}, u32[]{:S(2)}, u32[]{:S(2)}) collective-permute-start(bf16[64,1024]{1,0:T(8,128)(2,1)S(1)} %collective-permute-done.31), channel_id=1, source_target_pairs={{0,12},{1,13},{2,14},{3,15},{4,0},{5,1},{6,2},{7,3},{8,4},{9,5},{1... | collective-permute-start | bytes 393224 | tf_op jit(solution)/shard_map/ppermute | solution.py:63
  54.6 9.9 %collective-permute-start.6 = (bf16[2,32,512]{2,1,0:T(8,128)(2,1)S(1)}, bf16[2,32,512]{2,1,0:T(8,128)(2,1)S(1)}, u32[]{:S(2)}, u32[]{:S(2)}) collective-permute-start(bf16[2,32,512]{2,1,0:T(8,128)(2,1)S(1)} %pad_maximum_fusion.3), channel_id=1, source_target_pairs={{0,2},{1,3},{2,4},{3,5},{4,6},{5,7},{6,8},{7,9},{8,10},{9,11},{10,... | collective-permute-start | bytes 196616 | tf_op jit(solution)/shard_map/ppermute | solution.py:70
  64.5 16.0 %collective-permute-start.33 = (bf16[64,1024]{1,0:T(8,128)(2,1)S(1)}, bf16[64,1024]{1,0:T(8,128)(2,1)S(1)}, u32[]{:S(2)}, u32[]{:S(2)}) collective-permute-start(bf16[64,1024]{1,0:T(8,128)(2,1)S(1)} %collective-permute-done.31), channel_id=1, source_target_pairs={{0,4},{1,5},{2,6},{3,7},{4,8},{5,9},{6,10},{7,11},{8,12},{9,13},{1... | collective-permute-start | bytes 393224 | tf_op jit(solution)/shard_map/ppermute | solution.py:63
  64.6 10.8 %collective-permute-start.21 = (bf16[32,2048]{1,0:T(8,128)(2,1)S(1)}, bf16[32,2048]{1,0:T(8,128)(2,1)S(1)}, u32[]{:S(2)}, u32[]{:S(2)}) collective-permute-start(bf16[32,2048]{1,0:T(8,128)(2,1)S(1)} %get-tuple-element.69), channel_id=1, source_target_pairs={{0,64},{1,65},{2,66},{3,67},{4,68},{5,69},{6,70},{7,71},{8,72},{9,... | collective-permute-start | bytes 393224 | tf_op jit(solution)/shard_map/ppermute | solution.py:63
  65.5 29.7 %copy-start.2 = (f32[1024]{0:T(1024)S(1)}, f32[1024]{0:T(1024)}, u32[]{:S(2)}) copy-start(f32[1024]{0:T(1024)} %param.23) | copy-start | bytes 12292
  73.0 7.6 %collective-permute-start.22 = (bf16[32,2048]{1,0:T(8,128)(2,1)S(1)}, bf16[32,2048]{1,0:T(8,128)(2,1)S(1)}, u32[]{:S(2)}, u32[]{:S(2)}) collective-permute-start(bf16[32,2048]{1,0:T(8,128)(2,1)S(1)} %get-tuple-element.69), channel_id=1, source_target_pairs={{0,192},{1,193},{2,194},{3,195},{4,196},{5,197},{6,198},{7,199},{8... | collective-permute-start | bytes 393224 | tf_op jit(solution)/shard_map/ppermute | solution.py:63
  75.3 7.3 %collective-permute-start.34 = (bf16[64,1024]{1,0:T(8,128)(2,1)S(1)}, bf16[64,1024]{1,0:T(8,128)(2,1)S(1)}, u32[]{:S(2)}, u32[]{:S(2)}) collective-permute-start(bf16[64,1024]{1,0:T(8,128)(2,1)S(1)} %collective-permute-done.32), channel_id=1, source_target_pairs={{0,12},{1,13},{2,14},{3,15},{4,0},{5,1},{6,2},{7,3},{8,4},{9,5},{1... | collective-permute-start | bytes 393224 | tf_op jit(solution)/shard_map/ppermute | solution.py:63
  77.7 5.0 %collective-permute-start.23 = (bf16[32,2048]{1,0:T(8,128)(2,1)S(1)}, bf16[32,2048]{1,0:T(8,128)(2,1)S(1)}, u32[]{:S(2)}, u32[]{:S(2)}) collective-permute-start(bf16[32,2048]{1,0:T(8,128)(2,1)S(1)} %collective-permute-done.21), channel_id=1, source_target_pairs={{0,64},{1,65},{2,66},{3,67},{4,68},{5,69},{6,70},{7,71},{8,72},{9,... | collective-permute-start | bytes 393224 | tf_op jit(solution)/shard_map/ppermute | solution.py:63
  77.8 7.8 %collective-permute-start.14 = (bf16[2,32,2048]{2,1,0:T(8,128)(2,1)S(1)}, bf16[2,32,2048]{2,1,0:T(8,128)(2,1)S(1)}, u32[]{:S(2)}, u32[]{:S(2)}) collective-permute-start(bf16[2,32,2048]{2,1,0:T(8,128)(2,1)S(1)} %slice.30), channel_id=1, source_target_pairs={{0,192},{1,193},{2,194},{3,195},{4,196},{5,197},{6,198},{7,199},{8... | collective-permute-start | bytes 786440 | tf_op jit(solution)/shard_map/ppermute | solution.py:63
  80.5 7.9 %collective-permute-start.13 = (bf16[2,32,2048]{2,1,0:T(8,128)(2,1)S(1)}, bf16[2,32,2048]{2,1,0:T(8,128)(2,1)S(1)}, u32[]{:S(2)}, u32[]{:S(2)}) collective-permute-start(bf16[2,32,2048]{2,1,0:T(8,128)(2,1)S(1)} %slice.29), channel_id=1, source_target_pairs={{0,64},{1,65},{2,66},{3,67},{4,68},{5,69},{6,70},{7,71},{8,72},{9,... | collective-permute-start | bytes 786440 | tf_op jit(solution)/shard_map/ppermute | solution.py:63
  80.6 10.4 %collective-permute-start.15 = (bf16[4,32,2048]{2,1,0:T(8,128)(2,1)S(1)}, bf16[4,32,2048]{2,1,0:T(8,128)(2,1)S(1)}, u32[]{:S(2)}, u32[]{:S(2)}) collective-permute-start(bf16[4,32,2048]{2,1,0:T(8,128)(2,1)S(1)} %pad_maximum_fusion.refs_8_), channel_id=1, source_target_pairs={{0,2},{1,3},{2,0},{3,1},{4,6},{5,7},{6,4},{7,5},{8,10},{9,11},{10,... | collective-permute-start | bytes 1572872 | tf_op jit(solution)/shard_map/ppermute | solution.py:63
  82.6 11.1 %collective-permute-start.17 = (bf16[4,32,2048]{2,1,0:T(8,128)(2,1)S(1)}, bf16[4,32,2048]{2,1,0:T(8,128)(2,1)S(1)}, u32[]{:S(2)}, u32[]{:S(2)}) collective-permute-start(bf16[4,32,2048]{2,1,0:T(8,128)(2,1)S(1)} %collective-permute-done.12.refs_10_), channel_id=1, source_target_pairs={{0,2},{1,3},{2,0},{3,1},{4,6},{5,7},{6,4},{7,5},{8,10},{9,11},{10,... | collective-permute-start | bytes 1572872 | tf_op jit(solution)/shard_map/ppermute | solution.py:63
  82.8 12.5 %collective-permute-start.16 = (bf16[4,32,2048]{2,1,0:T(8,128)(2,1)S(1)}, bf16[4,32,2048]{2,1,0:T(8,128)(2,1)S(1)}, u32[]{:S(2)}, u32[]{:S(2)}) collective-permute-start(bf16[4,32,2048]{2,1,0:T(8,128)(2,1)S(1)} %collective-permute-done.11.refs_9_), channel_id=1, source_target_pairs={{0,2},{1,3},{2,0},{3,1},{4,6},{5,7},{6,4},{7,5},{8,10},{9,11},{10,... | collective-permute-start | bytes 1572872 | tf_op jit(solution)/shard_map/ppermute | solution.py:63
  85.6 5.6 %collective-permute-start.19 = (bf16[2,32,2048]{2,1,0:T(8,128)(2,1)S(1)}, bf16[2,32,2048]{2,1,0:T(8,128)(2,1)S(1)}, u32[]{:S(2)}, u32[]{:S(2)}) collective-permute-start(bf16[2,32,2048]{2,1,0:T(8,128)(2,1)S(1)} %collective-permute-done.14.refs_12_), channel_id=1, source_target_pairs={{0,2},{1,3},{2,0},{3,1},{4,6},{5,7},{6,4},{7,5},{8,10},{9,11},{10,... | collective-permute-start | bytes 786440 | tf_op jit(solution)/shard_map/ppermute | solution.py:63
  88.4 5.7 %collective-permute-start.18 = (bf16[2,32,2048]{2,1,0:T(8,128)(2,1)S(1)}, bf16[2,32,2048]{2,1,0:T(8,128)(2,1)S(1)}, u32[]{:S(2)}, u32[]{:S(2)}) collective-permute-start(bf16[2,32,2048]{2,1,0:T(8,128)(2,1)S(1)} %collective-permute-done.13.refs_11_), channel_id=1, source_target_pairs={{0,2},{1,3},{2,0},{3,1},{4,6},{5,7},{6,4},{7,5},{8,10},{9,11},{10,... | collective-permute-start | bytes 786440 | tf_op jit(solution)/shard_map/ppermute | solution.py:63
  91.0 18.7 %collective-permute-start.35 = (bf16[4,64,1024]{2,1,0:T(8,128)(2,1)S(1)}, bf16[4,64,1024]{2,1,0:T(8,128)(2,1)}, u32[]{:S(2)}, u32[]{:S(2)}) collective-permute-start(bf16[4,64,1024]{2,1,0:T(8,128)(2,1)S(1)} %pad_maximum_fusion.2.refs_12_), channel_id=1, source_target_pairs={{0,64},{1,65},{2,66},{3,67},{4,68},{5,69},{6,70},{7,71},{8,72},{9,... | collective-permute-start | bytes 1572872 | tf_op jit(solution)/shard_map/ppermute | solution.py:63
  91.1 20.3 %collective-permute-start.36 = (bf16[4,64,1024]{2,1,0:T(8,128)(2,1)S(1)}, bf16[4,64,1024]{2,1,0:T(8,128)(2,1)}, u32[]{:S(2)}, u32[]{:S(2)}) collective-permute-start(bf16[4,64,1024]{2,1,0:T(8,128)(2,1)S(1)} %pad_maximum_fusion.2.refs_12_), channel_id=1, source_target_pairs={{0,192},{1,193},{2,194},{3,195},{4,196},{5,197},{6,198},{7,199},{8... | collective-permute-start | bytes 1572872 | tf_op jit(solution)/shard_map/ppermute | solution.py:63
  93.8 16.1 %collective-permute-start.24 = (bf16[4,32,2048]{2,1,0:T(8,128)(2,1)S(1)}, bf16[4,32,2048]{2,1,0:T(8,128)(2,1)S(1)}, u32[]{:S(2)}, u32[]{:S(2)}) collective-permute-start(bf16[4,32,2048]{2,1,0:T(8,128)(2,1)S(1)} %pad_maximum_fusion.1.refs_4_), channel_id=1, source_target_pairs={{0,12},{1,13},{2,14},{3,15},{4,0},{5,1},{6,2},{7,3},{8,4},{9,5},{1... | collective-permute-start | bytes 1572872 | tf_op jit(solution)/shard_map/ppermute | solution.py:63
  94.1 18.8 %collective-permute-start.25 = (bf16[4,32,2048]{2,1,0:T(8,128)(2,1)S(1)}, bf16[4,32,2048]{2,1,0:T(8,128)(2,1)S(1)}, u32[]{:S(2)}, u32[]{:S(2)}) collective-permute-start(bf16[4,32,2048]{2,1,0:T(8,128)(2,1)S(1)} %pad_maximum_fusion.1.refs_4_), channel_id=1, source_target_pairs={{0,4},{1,5},{2,6},{3,7},{4,8},{5,9},{6,10},{7,11},{8,12},{9,13},{1... | collective-permute-start | bytes 1572872 | tf_op jit(solution)/shard_map/ppermute | solution.py:63
  109.8 14.0 %collective-permute-start.37 = (bf16[4,64,1024]{2,1,0:T(8,128)(2,1)}, bf16[4,64,1024]{2,1,0:T(8,128)(2,1)}, u32[]{:S(2)}, u32[]{:S(2)}) collective-permute-start(bf16[4,64,1024]{2,1,0:T(8,128)(2,1)} %collective-permute-done.35.refs_13_), channel_id=1, source_target_pairs={{0,64},{1,65},{2,66},{3,67},{4,68},{5,69},{6,70},{7,71},{8,72},{9,... | collective-permute-start | bytes 1572872 | tf_op jit(solution)/shard_map/ppermute | solution.py:63
  109.9 27.4 %collective-permute-start.26 = (bf16[4,32,2048]{2,1,0:T(8,128)(2,1)S(1)}, bf16[4,32,2048]{2,1,0:T(8,128)(2,1)S(1)}, u32[]{:S(2)}, u32[]{:S(2)}) collective-permute-start(bf16[4,32,2048]{2,1,0:T(8,128)(2,1)S(1)} %collective-permute-done.24.refs_5_), channel_id=1, source_target_pairs={{0,12},{1,13},{2,14},{3,15},{4,0},{5,1},{6,2},{7,3},{8,4},{9,5},{1... | collective-permute-start | bytes 1572872 | tf_op jit(solution)/shard_map/ppermute | solution.py:63
  111.5 28.2 %collective-permute-start.40 = (bf16[4,64,1024]{2,1,0:T(8,128)(2,1)}, bf16[4,64,1024]{2,1,0:T(8,128)(2,1)}, u32[]{:S(2)}, u32[]{:S(2)}) collective-permute-start(bf16[4,64,1024]{2,1,0:T(8,128)(2,1)} %collective-permute-done.36.refs_14_), channel_id=1, source_target_pairs={{0,2},{1,3},{2,0},{3,1},{4,6},{5,7},{6,4},{7,5},{8,10},{9,11},{10,... | collective-permute-start | bytes 1572872 | tf_op jit(solution)/shard_map/ppermute | solution.py:63
  112.8 27.2 %collective-permute-start.39 = (bf16[4,64,1024]{2,1,0:T(8,128)(2,1)}, bf16[4,64,1024]{2,1,0:T(8,128)(2,1)}, u32[]{:S(2)}, u32[]{:S(2)}) collective-permute-start(bf16[4,64,1024]{2,1,0:T(8,128)(2,1)} %collective-permute-done.35.refs_13_), channel_id=1, source_target_pairs={{0,2},{1,3},{2,0},{3,1},{4,6},{5,7},{6,4},{7,5},{8,10},{9,11},{10,... | collective-permute-start | bytes 1572872 | tf_op jit(solution)/shard_map/ppermute | solution.py:63
  112.8 27.3 %collective-permute-start.38 = (bf16[4,64,1024]{2,1,0:T(8,128)(2,1)S(1)}, bf16[4,64,1024]{2,1,0:T(8,128)(2,1)}, u32[]{:S(2)}, u32[]{:S(2)}) collective-permute-start(bf16[4,64,1024]{2,1,0:T(8,128)(2,1)S(1)} %pad_maximum_fusion.2.refs_12_), channel_id=1, source_target_pairs={{0,2},{1,3},{2,0},{3,1},{4,6},{5,7},{6,4},{7,5},{8,10},{9,11},{10,... | collective-permute-start | bytes 1572872 | tf_op jit(solution)/shard_map/ppermute | solution.py:63
  123.7 15.8 %collective-permute-start.20 = (bf16[2,64,512]{2,1,0:T(8,128)(2,1)S(1)}, bf16[2,64,512]{2,1,0:T(8,128)(2,1)S(1)}, u32[]{:S(2)}, u32[]{:S(2)}) collective-permute-start(bf16[2,64,512]{2,1,0:T(8,128)(2,1)S(1)} %get-tuple-element.67), channel_id=1, source_target_pairs={{0,1},{1,0},{2,3},{3,2},{4,5},{5,4},{6,7},{7,6},{8,9},{9,8},{10,11... | collective-permute-start | bytes 393224 | tf_op jit(solution)/shard_map/ppermute | solution.py:63
  137.3 4.6 %collective-permute-start.28 = (bf16[4,32,2048]{2,1,0:T(8,128)(2,1)S(1)}, bf16[4,32,2048]{2,1,0:T(8,128)(2,1)S(1)}, u32[]{:S(2)}, u32[]{:S(2)}) collective-permute-start(bf16[4,32,2048]{2,1,0:T(8,128)(2,1)S(1)} %collective-permute-done.24.refs_5_), channel_id=1, source_target_pairs={{0,2},{1,3},{2,0},{3,1},{4,6},{5,7},{6,4},{7,5},{8,10},{9,11},{10,... | collective-permute-start | bytes 1572872 | tf_op jit(solution)/shard_map/ppermute | solution.py:63
  139.6 2.3 %collective-permute-start.29 = (bf16[4,32,2048]{2,1,0:T(8,128)(2,1)S(1)}, bf16[4,32,2048]{2,1,0:T(8,128)(2,1)S(1)}, u32[]{:S(2)}, u32[]{:S(2)}) collective-permute-start(bf16[4,32,2048]{2,1,0:T(8,128)(2,1)S(1)} %collective-permute-done.25.refs_6_), channel_id=1, source_target_pairs={{0,2},{1,3},{2,0},{3,1},{4,6},{5,7},{6,4},{7,5},{8,10},{9,11},{10,... | collective-permute-start | bytes 1572872 | tf_op jit(solution)/shard_map/ppermute | solution.py:63
  139.7 2.9 %collective-permute-start.27 = (bf16[4,32,2048]{2,1,0:T(8,128)(2,1)S(1)}, bf16[4,32,2048]{2,1,0:T(8,128)(2,1)S(1)}, u32[]{:S(2)}, u32[]{:S(2)}) collective-permute-start(bf16[4,32,2048]{2,1,0:T(8,128)(2,1)S(1)} %pad_maximum_fusion.1.refs_4_), channel_id=1, source_target_pairs={{0,2},{1,3},{2,0},{3,1},{4,6},{5,7},{6,4},{7,5},{8,10},{9,11},{10,... | collective-permute-start | bytes 1572872 | tf_op jit(solution)/shard_map/ppermute | solution.py:63
  140.1 3.3 %collective-permute-start.41 = (bf16[4,64,1024]{2,1,0:T(8,128)(2,1)}, bf16[4,64,1024]{2,1,0:T(8,128)(2,1)S(1)}, u32[]{:S(2)}, u32[]{:S(2)}) collective-permute-start(bf16[4,64,1024]{2,1,0:T(8,128)(2,1)} %collective-permute-done.37.refs_15_), channel_id=1, source_target_pairs={{0,2},{1,3},{2,0},{3,1},{4,6},{5,7},{6,4},{7,5},{8,10},{9,11},{10,... | collective-permute-start | bytes 1572872 | tf_op jit(solution)/shard_map/ppermute | solution.py:63
  140.2 3.9 %collective-permute-start.30 = (bf16[4,32,2048]{2,1,0:T(8,128)(2,1)S(1)}, bf16[4,32,2048]{2,1,0:T(8,128)(2,1)S(1)}, u32[]{:S(2)}, u32[]{:S(2)}) collective-permute-start(bf16[4,32,2048]{2,1,0:T(8,128)(2,1)S(1)} %collective-permute-done.26.refs_7_), channel_id=1, source_target_pairs={{0,2},{1,3},{2,0},{3,1},{4,6},{5,7},{6,4},{7,5},{8,10},{9,11},{10,... | collective-permute-start | bytes 1572872 | tf_op jit(solution)/shard_map/ppermute | solution.py:63
  143.3 0.8 copy-start.5
  158.1 29.1 %collective-permute-start.42 = (bf16[2,256,512]{2,1,0:T(8,128)(2,1)}, bf16[2,256,512]{2,1,0:T(8,128)(2,1)S(1)}, u32[]{:S(2)}, u32[]{:S(2)}) collective-permute-start(bf16[2,256,512]{2,1,0:T(8,128)(2,1)} %get-tuple-element.64), channel_id=1, source_target_pairs={{0,1},{1,0},{2,3},{3,2},{4,5},{5,4},{6,7},{7,6},{8,9},{9,8},{10,11... | collective-permute-start | bytes 1572872 | tf_op jit(solution)/shard_map/ppermute | solution.py:63
where the time goes:
time: 189 us; the launch traced here: 188 us
  starting transfers between devices  80.1 us (42%)
  Pallas kernels  55.6 us (29%)
  waiting for transfers between devices  45.4 us (24%)
  local copies, waits for them, and re-layouts  4.14 us (2%)
  other arithmetic  2.08 us (1%)
    ppermute x39, starting transfers between devices, moved(): return lax.ppermute(array, AXES, route(STEPS[axis, by]))  69.8 us
    pallas_call x6, Pallas kernels, call(): pl.pallas_call(kernel, grid_spec=spec, out_shape=out_shape, compiler_para...  55.6 us
    ppermute x39, waiting for transfers between devices, moved(): return lax.ppermute(array, AXES, route(STEPS[axis, by]))  45.4 us
    ppermute x4, starting transfers between devices, along_frames(): return lax.ppermute(array, AXES, pairs)  10.3 us
  transfers between devices with their start and end apart: 43, of which 8 were waited for; matrix products, arithmetic and copies ran while one was open for 2% of the time, Pallas kernels for 21%

commit v1 on v0

--- a/solution.py
+++ b/solution.py
@@ -252,6 +252,8 @@
             rows = pl.ds(pl.multiple_of(at * 32, 32), 32)
             src = parts[r].at[j, :, : 3 * HALF]
             pltpu.make_async_copy(src, wqkv.at[rows], sem.at[0]).start()
+
+        def fetch_out(r, j, at):
             few = pl.ds(pl.multiple_of(at * 16, 16), 16)
             for s in range(2):
                 src = parts[r].at[j, 16 * s : 16 * s + 16, 3 * HALF :]
@@ -259,19 +261,24 @@
                 pltpu.make_async_copy(src, dst, sem.at[1]).start()
 
         each_piece("y", -1, where, True, fetch)
+        each_piece("y", -1, where, True, fetch_out)
 
     mine = dot(ctx_own[0], wo_own[...]).astype(bf16).astype(f32)
 
     @pl.when(u == 0)
     def _():
         pltpu.make_async_copy(wqkv, wqkv, sem.at[0]).wait()
-        pltpu.make_async_copy(wo, wo, sem.at[1]).wait()
 
     wk, wv = wqkv.at[:, HALF : 2 * HALF], wqkv.at[:, 2 * HALF :]
     project(n, wqkv.at[:, :HALF], wk, wv, q, k, v)
     mk[...] = dot(nm[0], wk[...]).astype(bf16)
     mv[...] = dot(nm[0], wv[...]).astype(bf16)
     attend(sc, u, begins, q, k, v, mk, mv, ctx)
+
+    @pl.when(u == 0)
+    def _():
+        pltpu.make_async_copy(wo, wo, sem.at[1]).wait()
+
     theirs = dot(ctx[0], wo[...]).astype(bf16).astype(f32)
     both = mine + theirs
     seg = sc[3] * S + lax.broadcasted_iota(i32, (S, 1), 0)
@@ -305,39 +312,39 @@
     wu, wd, acc, sem = refs[22:]
     where = (sc[4], sc[6], sc[5])
 
-    def fetch_up(i):
+    x = sc[4]
+
+    def fetch_up(i, carry):
+        ahead = jnp.where(i == 0, 0, jnp.where(i == 1, -1, jnp.where(i == 2, 1, 2)))
+        chunk = (x + ahead) & 3
+        cols = pl.ds(pl.multiple_of(chunk * HALF, HALF), HALF)
+
         def fetch(r, j, at):
             rows = pl.ds(pl.multiple_of(at * 32, 32), 32)
-            cols = pl.ds(pl.multiple_of(i * HALF, HALF), HALF)
             pltpu.make_async_copy(ups[r].at[j, :, cols], wu.at[i, rows], sem.at[i]).start()
 
         each_piece("x", 1, where, False, fetch)
+        return carry
 
     def fetch_down(r, j, at):
-        rows = pl.ds(pl.multiple_of(at * 64, 64), 64)
-        pltpu.make_async_copy(downs[r].at[j], wd.at[rows], sem.at[4]).start()
-
-    fetch_up(0)
+        rows = pl.ds(pl.multiple_of((at & 7) * 64, 64), 64)
+        slot = r % 4
+        copy = pltpu.make_async_copy(downs[r].at[j], wd.at[slot, rows], sem.at[4 + slot])
+        copy.start()
+
+    fetch_up(0, 0)
     each_piece("y", -1, where, False, fetch_down)
-
-    def fetch_rest(i, carry):
-        fetch_up(i)
-        return carry
-
-    lax.fori_loop(1, 4, fetch_rest, 0)
+    lax.fori_loop(1, 4, fetch_up, 0)
+    acc[...] = jnp.zeros_like(acc)
 
     def step(i, carry):
         pltpu.make_async_copy(wu.at[i], wu.at[i], sem.at[i]).wait()
-
-        @pl.when(i == 0)
-        def _():
-            pltpu.make_async_copy(wd, wd, sem.at[4]).wait()
-            acc[...] = jnp.zeros_like(acc)
+        pltpu.make_async_copy(wd.at[i], wd.at[i], sem.at[4 + i]).wait()
 
         def some(r, carry):
             rows = pl.ds(pl.multiple_of(r * F, F), F)
             hidden = gelu(dot(nf[rows], wu[i])).astype(bf16)
-            acc[rows] += dot(hidden, wd[pl.ds(pl.multiple_of(i * HALF, HALF), HALF)])
+            acc[rows] += dot(hidden, wd[i])
             return carry
 
         return lax.fori_loop(0, U, some, carry)
@@ -571,9 +578,9 @@
         arrays((U, F, HALF), (U, F, HALF)),
         [
             pltpu.VMEM((4, D, HALF), bf16),
-            pltpu.VMEM((2048, D), bf16),
+            pltpu.VMEM((4, HALF, D), bf16),
             pltpu.VMEM((rows, D), f32),
-            pltpu.SemaphoreType.DMA((5,)),
+            pltpu.SemaphoreType.DMA((8,)),
         ],
         4 << 30,
         (stored(nf), stored(hid), stored(own), *ups, *downs),

time: 189 us -> 189 us (level)
  no operation moved by 1% of the time
where the time goes in v1:
time: 189 us
  starting transfers between devices  80.1 us (42%)
  Pallas kernels  55.8 us (30%)
  waiting for transfers between devices  45.4 us (24%)
  local copies, waits for them, and re-layouts  4.14 us (2%)
  other arithmetic  2.08 us (1%)
    ppermute x39, starting transfers between devices, moved(): return lax.ppermute(array, AXES, route(STEPS[axis, by]))  69.8 us
    pallas_call x6, Pallas kernels, call(): pl.pallas_call(kernel, grid_spec=spec, out_shape=out_shape, compiler_para...  55.8 us
    ppermute x39, waiting for transfers between devices, moved(): return lax.ppermute(array, AXES, route(STEPS[axis, by]))  45.4 us
    ppermute x4, starting transfers between devices, along_frames(): return lax.ppermute(array, AXES, pairs)  10.3 us
  transfers between devices with their start and end apart: 43, of which 8 were waited for; matrix products, arithmetic and copies ran while one was open for 2% of the time, Pallas kernels for 21%

profile of v1, /device:TPU:1, one launch (start us, length us, event | category | flops | bytes accessed | tf_op | source)
XLA Modules:
  0.0 188.6 jit_solution(12966422126255276824)
XLA Ops:
  0.7 0.9 constant_dynamic-slice_fusion.5
  1.6 0.7 dynamic_slice.18
  2.4 0.1 concatenate.15.sc.refs_0_
  2.4 1.7 shard_map.140
  4.2 7.8 %collective-permute-start.7 = (bf16[32,2048]{1,0:T(8,128)(2,1)S(1)}, bf16[32,2048]{1,0:T(8,128)(2,1)S(1)}, u32[]{:S(2)}, u32[]{:S(2)}) collective-permute-start(bf16[32,2048]{1,0:T(8,128)(2,1)S(1)} %get-tuple-element.44), channel_id=1, source_target_pairs={{0,1},{1,0},{2,3},{3,2},{4,5},{5,4},{6,7},{7,6},{8,9},{9,8},{10,11... | collective-permute-start | bytes 393224 | tf_op jit(solution)/shard_map/ppermute | solution.py:63
  12.0 0.1 collective-permute-start.2
  12.1 5.3 %collective-permute-start.4 = (bf16[32,4096]{1,0:T(8,128)(2,1)S(1)}, bf16[32,4096]{1,0:T(8,128)(2,1)S(1)}, u32[]{:S(2)}, u32[]{:S(2)}) collective-permute-start(bf16[32,4096]{1,0:T(8,128)(2,1)S(1)} %get-tuple-element.35), channel_id=1, source_target_pairs={{0,1},{1,0},{2,3},{3,2},{4,5},{5,4},{6,7},{7,6},{8,9},{9,8},{10,11... | collective-permute-start | bytes 786440 | tf_op jit(solution)/shard_map/ppermute | solution.py:63
  17.3 0.7 copy.16
  18.0 0.7 reshape.13.fb
  18.7 4.6 %collective-permute-start = (bf16[2,32,320]{2,1,0:T(8,128)(2,1)S(1)}, bf16[2,32,320]{2,1,0:T(8,128)(2,1)S(1)}, u32[]{:S(2)}, u32[]{:S(2)}) collective-permute-start(bf16[2,32,320]{2,1,0:T(8,128)(2,1)S(1)} %constant_dynamic-slice_fusion), channel_id=1, source_target_pairs={{0,2},{1,3},{2,4},{3,5},{4,6},{5,7},{6,8},{7,9},{8,10},{9,11},{10,... | collective-permute-start | bytes 122888 | tf_op jit(solution)/shard_map/ppermute | solution.py:70
  23.4 1.9 %collective-permute-start.8 = (bf16[32,2048]{1,0:T(8,128)(2,1)S(1)}, bf16[32,2048]{1,0:T(8,128)(2,1)S(1)}, u32[]{:S(2)}, u32[]{:S(2)}) collective-permute-start(bf16[32,2048]{1,0:T(8,128)(2,1)S(1)} %collective-permute-done.7), channel_id=1, source_target_pairs={{0,12},{1,13},{2,14},{3,15},{4,0},{5,1},{6,2},{7,3},{8,4},{9,5},{1... | collective-permute-start | bytes 393224 | tf_op jit(solution)/shard_map/ppermute | solution.py:63
  25.3 1.9 %collective-permute-start.1 = (bf16[2,16,320]{2,1,0:T(8,128)(2,1)S(1)}, bf16[2,16,320]{2,1,0:T(8,128)(2,1)S(1)}, u32[]{:S(2)}, u32[]{:S(2)}) collective-permute-start(bf16[2,16,320]{2,1,0:T(8,128)(2,1)S(1)} %constant_dynamic-slice_fusion.4), channel_id=1, source_target_pairs={{2,0},{3,1},{4,2},{5,3},{6,4},{7,5},{8,6},{9,7},{10,8},{11,9},{12,... | collective-permute-start | bytes 61448 | tf_op jit(solution)/shard_map/ppermute | solution.py:70
  27.2 0.9 constant_dynamic-slice_fusion.3
  28.0 3.7 %collective-permute-done.4.mem_b = bf16[32,4096]{1,0:T(8,128)(2,1)S(1)} collective-permute-done((bf16[32,4096]{1,0:T(8,128)(2,1)S(1)}, bf16[32,4096]{1,0:T(8,128)(2,1)S(1)}, u32[]{:S(2)}, u32[]{:S(2)}) %collective-permute-start.4) | collective-permute-done | bytes 262176 | tf_op jit(solution)/shard_map/ppermute | solution.py:63
  31.7 1.3 collective-permute-start.9
  33.0 4.5 %collective-permute-start.10 = (bf16[32,2048]{1,0:T(8,128)(2,1)S(1)}, bf16[32,2048]{1,0:T(8,128)(2,1)S(1)}, u32[]{:S(2)}, u32[]{:S(2)}) collective-permute-start(bf16[32,2048]{1,0:T(8,128)(2,1)S(1)} %collective-permute-done.8), channel_id=1, source_target_pairs={{0,12},{1,13},{2,14},{3,15},{4,0},{5,1},{6,2},{7,3},{8,4},{9,5},{1... | collective-permute-start | bytes 393224 | tf_op jit(solution)/shard_map/ppermute | solution.py:63
  37.6 5.9 %collective-permute-start.31 = (bf16[64,1024]{1,0:T(8,128)(2,1)S(1)}, bf16[64,1024]{1,0:T(8,128)(2,1)S(1)}, u32[]{:S(2)}, u32[]{:S(2)}) collective-permute-start(bf16[64,1024]{1,0:T(8,128)(2,1)S(1)} %get-tuple-element.57), channel_id=1, source_target_pairs={{0,1},{1,0},{2,3},{3,2},{4,5},{5,4},{6,7},{7,6},{8,9},{9,8},{10,11... | collective-permute-start | bytes 393224 | tf_op jit(solution)/shard_map/ppermute | solution.py:63
  43.5 2.8 %collective-permute-start.3 = (bf16[320,256]{1,0:T(8,128)(2,1)S(1)}, bf16[320,256]{1,0:T(8,128)(2,1)S(1)}, u32[]{:S(2)}, u32[]{:S(2)}) collective-permute-start(bf16[320,256]{1,0:T(8,128)(2,1)S(1)} %collective-permute-done.2.wf_a), channel_id=1, source_target_pairs={{0,2},{1,3},{2,0},{3,1},{4,6},{5,7},{6,4},{7,5},{8,10},{9,11},{10,... | collective-permute-start | bytes 491528 | tf_op jit(solution)/shard_map/ppermute | solution.py:63
  46.4 0.1 pad_maximum_fusion.refs_8_
  46.4 2.6 %collective-permute-start.12 = (bf16[4,32,2048]{2,1,0:T(8,128)(2,1)S(1)}, bf16[4,32,2048]{2,1,0:T(8,128)(2,1)S(1)}, u32[]{:S(2)}, u32[]{:S(2)}) collective-permute-start(bf16[4,32,2048]{2,1,0:T(8,128)(2,1)S(1)} %pad_maximum_fusion.refs_8_), channel_id=1, source_target_pairs={{0,192},{1,193},{2,194},{3,195},{4,196},{5,197},{6,198},{7,199},{8... | collective-permute-start | bytes 1572872 | tf_op jit(solution)/shard_map/ppermute | solution.py:63
  49.0 0.1 collective-permute-start.11
  49.1 1.9 %collective-permute-start.5 = (bf16[2,32,512]{2,1,0:T(8,128)(2,1)S(1)}, bf16[2,32,512]{2,1,0:T(8,128)(2,1)S(1)}, u32[]{:S(2)}, u32[]{:S(2)}) collective-permute-start(bf16[2,32,512]{2,1,0:T(8,128)(2,1)S(1)} %constant_dynamic-slice_fusion.3), channel_id=1, source_target_pairs={{0,2},{1,3},{2,4},{3,5},{4,6},{5,7},{6,8},{7,9},{8,10},{9,11},{10,... | collective-permute-start | bytes 196616 | tf_op jit(solution)/shard_map/ppermute | solution.py:70
  51.1 3.6 %collective-permute-start.32 = (bf16[64,1024]{1,0:T(8,128)(2,1)S(1)}, bf16[64,1024]{1,0:T(8,128)(2,1)S(1)}, u32[]{:S(2)}, u32[]{:S(2)}) collective-permute-start(bf16[64,1024]{1,0:T(8,128)(2,1)S(1)} %collective-permute-done.31), channel_id=1, source_target_pairs={{0,12},{1,13},{2,14},{3,15},{4,0},{5,1},{6,2},{7,3},{8,4},{9,5},{1... | collective-permute-start | bytes 393224 | tf_op jit(solution)/shard_map/ppermute | solution.py:63
  54.6 1.9 %collective-permute-start.6 = (bf16[2,32,512]{2,1,0:T(8,128)(2,1)S(1)}, bf16[2,32,512]{2,1,0:T(8,128)(2,1)S(1)}, u32[]{:S(2)}, u32[]{:S(2)}) collective-permute-start(bf16[2,32,512]{2,1,0:T(8,128)(2,1)S(1)} %pad_maximum_fusion.3), channel_id=1, source_target_pairs={{0,2},{1,3},{2,4},{3,5},{4,6},{5,7},{6,8},{7,9},{8,10},{9,11},{10,... | collective-permute-start | bytes 196616 | tf_op jit(solution)/shard_map/ppermute | solution.py:70
  56.6 7.9 %shard_map.141 = (bf16[2,256,1024]{2,1,0:T(8,128)(2,1)}, bf16[2,384,1024]{2,1,0:T(8,128)(2,1)}, bf16[2,320,512]{2,1,0:T(8,128)(2,1)}, bf16[2,320,512]{2,1,0:T(8,128)(2,1)}, bf16[2,320,512]{2,1,0:T(8,128)(2,1)}) custom-call(s32[8]{0:T(128)S(1)} %concatenate.15.sc.refs_0_, bf16[4,256,320]{2,1,0:T(8,128)(2,1)S(1)} %reshape.13.fb, ...), custom_call_target="tpu_custom_call" | custom-call | flops 2013265920 | bytes 8388608 | tf_op jit(solution)/shard_map/pallas_call | solution.py:397
  64.6 1.0 collective-permute-start.21
  65.6 7.4 %shard_map.142 = (bf16[2,320,512]{2,1,0:T(8,128)(2,1)}, bf16[2,96,1024]{2,1,0:T(8,128)(2,1)}) custom-call(s32[8]{0:T(128)S(1)} %concatenate.15.sc.refs_0_, bf16[4,64,512]{2,1,0:T(8,128)(2,1)} %mem_a.1, bf16[32,4096]{1,0:T(8,128)(2,1)S(1)} %collective-permute-done.4.mem_b, bf16[2,32,512]{2,1,0:T(8,128)(2,1)S(1)} %collective-permute-done.5.halo_a, ...), custom_call_target="tpu_custom_call" | custom-call | flops 2147483648 | bytes 8388608 | tf_op jit(solution)/shard_map/pallas_call | solution.py:397
  73.0 2.3 %collective-permute-start.22 = (bf16[32,2048]{1,0:T(8,128)(2,1)S(1)}, bf16[32,2048]{1,0:T(8,128)(2,1)S(1)}, u32[]{:S(2)}, u32[]{:S(2)}) collective-permute-start(bf16[32,2048]{1,0:T(8,128)(2,1)S(1)} %get-tuple-element.69), channel_id=1, source_target_pairs={{0,192},{1,193},{2,194},{3,195},{4,196},{5,197},{6,198},{7,199},{8... | collective-permute-start | bytes 393224 | tf_op jit(solution)/shard_map/ppermute | solution.py:63
  75.3 2.4 %collective-permute-start.34 = (bf16[64,1024]{1,0:T(8,128)(2,1)S(1)}, bf16[64,1024]{1,0:T(8,128)(2,1)S(1)}, u32[]{:S(2)}, u32[]{:S(2)}) collective-permute-start(bf16[64,1024]{1,0:T(8,128)(2,1)S(1)} %collective-permute-done.32), channel_id=1, source_target_pairs={{0,12},{1,13},{2,14},{3,15},{4,0},{5,1},{6,2},{7,3},{8,4},{9,5},{1... | collective-permute-start | bytes 393224 | tf_op jit(solution)/shard_map/ppermute | solution.py:63
  77.8 2.8 %collective-permute-start.14 = (bf16[2,32,2048]{2,1,0:T(8,128)(2,1)S(1)}, bf16[2,32,2048]{2,1,0:T(8,128)(2,1)S(1)}, u32[]{:S(2)}, u32[]{:S(2)}) collective-permute-start(bf16[2,32,2048]{2,1,0:T(8,128)(2,1)S(1)} %slice.30), channel_id=1, source_target_pairs={{0,192},{1,193},{2,194},{3,195},{4,196},{5,197},{6,198},{7,199},{8... | collective-permute-start | bytes 786440 | tf_op jit(solution)/shard_map/ppermute | solution.py:63
  80.5 0.1 collective-permute-start.13
  80.6 2.0 %collective-permute-start.15 = (bf16[4,32,2048]{2,1,0:T(8,128)(2,1)S(1)}, bf16[4,32,2048]{2,1,0:T(8,128)(2,1)S(1)}, u32[]{:S(2)}, u32[]{:S(2)}) collective-permute-start(bf16[4,32,2048]{2,1,0:T(8,128)(2,1)S(1)} %pad_maximum_fusion.refs_8_), channel_id=1, source_target_pairs={{0,2},{1,3},{2,0},{3,1},{4,6},{5,7},{6,4},{7,5},{8,10},{9,11},{10,... | collective-permute-start | bytes 1572872 | tf_op jit(solution)/shard_map/ppermute | solution.py:63
  82.6 0.1 collective-permute-start.17
  82.8 2.8 %collective-permute-start.16 = (bf16[4,32,2048]{2,1,0:T(8,128)(2,1)S(1)}, bf16[4,32,2048]{2,1,0:T(8,128)(2,1)S(1)}, u32[]{:S(2)}, u32[]{:S(2)}) collective-permute-start(bf16[4,32,2048]{2,1,0:T(8,128)(2,1)S(1)} %collective-permute-done.11.refs_9_), channel_id=1, source_target_pairs={{0,2},{1,3},{2,0},{3,1},{4,6},{5,7},{6,4},{7,5},{8,10},{9,11},{10,... | collective-permute-start | bytes 1572872 | tf_op jit(solution)/shard_map/ppermute | solution.py:63
  85.6 1.5 collective-permute-start.19
  87.0 1.4 collective-permute-done.13.refs_11_
  88.4 2.5 %collective-permute-start.18 = (bf16[2,32,2048]{2,1,0:T(8,128)(2,1)S(1)}, bf16[2,32,2048]{2,1,0:T(8,128)(2,1)S(1)}, u32[]{:S(2)}, u32[]{:S(2)}) collective-permute-start(bf16[2,32,2048]{2,1,0:T(8,128)(2,1)S(1)} %collective-permute-done.13.refs_11_), channel_id=1, source_target_pairs={{0,2},{1,3},{2,0},{3,1},{4,6},{5,7},{6,4},{7,5},{8,10},{9,11},{10,... | collective-permute-start | bytes 786440 | tf_op jit(solution)/shard_map/ppermute | solution.py:63
  90.9 0.1 pad_maximum_fusion.1.refs_4_
  91.0 0.1 collective-permute-start.35
  91.1 2.7 %collective-permute-start.36 = (bf16[4,64,1024]{2,1,0:T(8,128)(2,1)S(1)}, bf16[4,64,1024]{2,1,0:T(8,128)(2,1)}, u32[]{:S(2)}, u32[]{:S(2)}) collective-permute-start(bf16[4,64,1024]{2,1,0:T(8,128)(2,1)S(1)} %pad_maximum_fusion.2.refs_12_), channel_id=1, source_target_pairs={{0,192},{1,193},{2,194},{3,195},{4,196},{5,197},{6,198},{7,199},{8... | collective-permute-start | bytes 1572872 | tf_op jit(solution)/shard_map/ppermute | solution.py:63
  93.8 0.3 collective-permute-start.24
  94.1 1.2 collective-permute-start.25
  95.3 14.7 %shard_map.143 = (bf16[512,1024]{1,0:T(8,128)(2,1)}, bf16[512,1024]{1,0:T(8,128)(2,1)}, bf16[2,64,1024]{2,1,0:T(8,128)(2,1)S(1)}) custom-call(s32[8]{0:T(128)S(1)} %concatenate.15.sc.refs_0_, bf16[2,384,1024]{2,1,0:T(8,128)(2,1)} %get-tuple-element.37.refs_1_, bf16[2,96,1024]{2,1,0:T(8,128)(2,1)} %get-tuple-element.41.refs_2_, s32[4,64]{1,0:T(4,128)S(1)} %copy-done.3, ...), custom_call_target="tpu_custom_call" | custom-call | flops 6442450944 | bytes 8388608 | tf_op jit(solution)/shard_map/pallas_call | solution.py:397
  110.0 0.1 collective-permute-start.37
  110.1 1.6 collective-permute-start.26
  111.7 1.4 collective-permute-start.40
  113.1 0.5 collective-permute-start.38
  113.6 10.4 %collective-permute-done.37.refs_15_ = bf16[4,64,1024]{2,1,0:T(8,128)(2,1)} collective-permute-done((bf16[4,64,1024]{2,1,0:T(8,128)(2,1)}, bf16[4,64,1024]{2,1,0:T(8,128)(2,1)}, u32[]{:S(2)}, u32[]{:S(2)}) %collective-permute-start.37) | collective-permute-done | bytes 524320 | tf_op jit(solution)/shard_map/ppermute | solution.py:63
  124.0 3.5 %collective-permute-start.20 = (bf16[2,64,512]{2,1,0:T(8,128)(2,1)S(1)}, bf16[2,64,512]{2,1,0:T(8,128)(2,1)S(1)}, u32[]{:S(2)}, u32[]{:S(2)}) collective-permute-start(bf16[2,64,512]{2,1,0:T(8,128)(2,1)S(1)} %get-tuple-element.67), channel_id=1, source_target_pairs={{0,1},{1,0},{2,3},{3,2},{4,5},{5,4},{6,7},{7,6},{8,9},{9,8},{10,11... | collective-permute-start | bytes 393224 | tf_op jit(solution)/shard_map/ppermute | solution.py:63
  127.5 10.0 %shard_map.144.refs_3_ = bf16[512,1024]{1,0:T(8,128)(2,1)} custom-call(bf16[512,1024]{1,0:T(8,128)(2,1)} %get-tuple-element.48.nf.refs_1_, bf16[1024,2048]{1,0:T(8,128)(2,1)} %wu.3, bf16[2048,1024]{1,0:T(8,128)(2,1)} %wd.3), custom_call_target="tpu_custom_call" | custom-call | flops 4294967296 | bytes 8388608 | tf_op jit(solution)/shard_map/pallas_call | solution.py:397
  137.5 2.3 %collective-permute-start.28 = (bf16[4,32,2048]{2,1,0:T(8,128)(2,1)S(1)}, bf16[4,32,2048]{2,1,0:T(8,128)(2,1)S(1)}, u32[]{:S(2)}, u32[]{:S(2)}) collective-permute-start(bf16[4,32,2048]{2,1,0:T(8,128)(2,1)S(1)} %collective-permute-done.24.refs_5_), channel_id=1, source_target_pairs={{0,2},{1,3},{2,0},{3,1},{4,6},{5,7},{6,4},{7,5},{8,10},{9,11},{10,... | collective-permute-start | bytes 1572872 | tf_op jit(solution)/shard_map/ppermute | solution.py:63
  139.8 0.1 collective-permute-start.29
  139.9 0.4 collective-permute-start.27
  140.3 0.1 collective-permute-start.41
  140.4 0.4 collective-permute-start.30
  140.8 1.2 collective-permute-done.29.refs_10_
  142.1 0.7 collective-permute-done.27.refs_8_
  142.8 0.7 collective-permute-done.41.refs_19_
  143.6 0.7 collective-permute-done.30.refs_11_
  144.4 14.0 %shard_map.145 = (bf16[2,256,512]{2,1,0:T(8,128)(2,1)S(1)}, bf16[2,256,512]{2,1,0:T(8,128)(2,1)}) custom-call(s32[8]{0:T(128)S(1)} %concatenate.15.sc.refs_0_, bf16[512,1024]{1,0:T(8,128)(2,1)} %get-tuple-element.48.nf.refs_1_, bf16[512,1024]{1,0:T(8,128)(2,1)} %get-tuple-element.51.refs_2_, bf16[512,1024]{1,0:T(8,128)(2,1)} %shard_map.144.refs_3_, ...), custom_call_target="tpu_custom_call" | custom-call | flops 4294967296 | bytes 8388608 | tf_op jit(solution)/shard_map/pallas_call | solution.py:397
  158.4 1.9 %collective-permute-start.42 = (bf16[2,256,512]{2,1,0:T(8,128)(2,1)}, bf16[2,256,512]{2,1,0:T(8,128)(2,1)S(1)}, u32[]{:S(2)}, u32[]{:S(2)}) collective-permute-start(bf16[2,256,512]{2,1,0:T(8,128)(2,1)} %get-tuple-element.64), channel_id=1, source_target_pairs={{0,1},{1,0},{2,3},{3,2},{4,5},{5,4},{6,7},{7,6},{8,9},{9,8},{10,11... | collective-permute-start | bytes 1572872 | tf_op jit(solution)/shard_map/ppermute | solution.py:63
  160.3 0.7 maximum_select_fusion.1
  161.1 26.4 %collective-permute-done.42 = bf16[2,256,512]{2,1,0:T(8,128)(2,1)S(1)} collective-permute-done((bf16[2,256,512]{2,1,0:T(8,128)(2,1)}, bf16[2,256,512]{2,1,0:T(8,128)(2,1)S(1)}, u32[]{:S(2)}, u32[]{:S(2)}) %collective-permute-start.42) | collective-permute-done | bytes 524320 | tf_op jit(solution)/shard_map/ppermute | solution.py:63
  187.5 1.1 maximum_select_fusion
  (59 shorter events, 0.4 us)
Async XLA Ops:
  2.4 14.9 %copy-start.4 = (bf16[4,1024,80]{1,2,0:T(8,128)(2,1)S(1)}, bf16[4,1024,80]{1,2,0:T(8,128)(2,1)}, u32[]{:S(2)}) copy-start(bf16[4,1024,80]{1,2,0:T(8,128)(2,1)} %param.13) | copy-start | bytes 1966084
  4.1 52.4 %copy-start = (bf16[320,512]{1,0:T(8,128)(2,1)S(1)}, bf16[320,512]{1,0:T(8,128)(2,1)}, u32[]{:S(2)}) copy-start(bf16[320,512]{1,0:T(8,128)(2,1)} %wf_own.1) | copy-start | bytes 983044
  4.1 52.4 %copy-start.1 = (f32[1024]{0:T(1024)S(1)}, f32[1024]{0:T(1024)}, u32[]{:S(2)}) copy-start(f32[1024]{0:T(1024)} %param.18) | copy-start | bytes 12292
  4.2 19.2 %collective-permute-start.7 = (bf16[32,2048]{1,0:T(8,128)(2,1)S(1)}, bf16[32,2048]{1,0:T(8,128)(2,1)S(1)}, u32[]{:S(2)}, u32[]{:S(2)}) collective-permute-start(bf16[32,2048]{1,0:T(8,128)(2,1)S(1)} %get-tuple-element.44), channel_id=1, source_target_pairs={{0,1},{1,0},{2,3},{3,2},{4,5},{5,4},{6,7},{7,6},{8,9},{9,8},{10,11... | collective-permute-start | bytes 393224 | tf_op jit(solution)/shard_map/ppermute | solution.py:63
  12.0 25.6 %collective-permute-start.2 = (bf16[320,256]{1,0:T(8,128)(2,1)S(1)}, bf16[320,256]{1,0:T(8,128)(2,1)S(1)}, u32[]{:S(2)}, u32[]{:S(2)}) collective-permute-start(bf16[320,256]{1,0:T(8,128)(2,1)S(1)} %constant_dynamic-slice_fusion.5), channel_id=1, source_target_pairs={{0,1},{1,0},{2,3},{3,2},{4,5},{5,4},{6,7},{7,6},{8,9},{9,8},{10,11... | collective-permute-start | bytes 491528 | tf_op jit(solution)/shard_map/ppermute | solution.py:63
  12.1 19.7 %collective-permute-start.4 = (bf16[32,4096]{1,0:T(8,128)(2,1)S(1)}, bf16[32,4096]{1,0:T(8,128)(2,1)S(1)}, u32[]{:S(2)}, u32[]{:S(2)}) collective-permute-start(bf16[32,4096]{1,0:T(8,128)(2,1)S(1)} %get-tuple-element.35), channel_id=1, source_target_pairs={{0,1},{1,0},{2,3},{3,2},{4,5},{5,4},{6,7},{7,6},{8,9},{9,8},{10,11... | collective-permute-start | bytes 786440 | tf_op jit(solution)/shard_map/ppermute | solution.py:63
  18.7 30.4 %collective-permute-start = (bf16[2,32,320]{2,1,0:T(8,128)(2,1)S(1)}, bf16[2,32,320]{2,1,0:T(8,128)(2,1)S(1)}, u32[]{:S(2)}, u32[]{:S(2)}) collective-permute-start(bf16[2,32,320]{2,1,0:T(8,128)(2,1)S(1)} %constant_dynamic-slice_fusion), channel_id=1, source_target_pairs={{0,2},{1,3},{2,4},{3,5},{4,6},{5,7},{6,8},{7,9},{8,10},{9,11},{10,... | collective-permute-start | bytes 122888 | tf_op jit(solution)/shard_map/ppermute | solution.py:70
  23.4 9.7 %collective-permute-start.8 = (bf16[32,2048]{1,0:T(8,128)(2,1)S(1)}, bf16[32,2048]{1,0:T(8,128)(2,1)S(1)}, u32[]{:S(2)}, u32[]{:S(2)}) collective-permute-start(bf16[32,2048]{1,0:T(8,128)(2,1)S(1)} %collective-permute-done.7), channel_id=1, source_target_pairs={{0,12},{1,13},{2,14},{3,15},{4,0},{5,1},{6,2},{7,3},{8,4},{9,5},{1... | collective-permute-start | bytes 393224 | tf_op jit(solution)/shard_map/ppermute | solution.py:63
  25.3 23.7 %collective-permute-start.1 = (bf16[2,16,320]{2,1,0:T(8,128)(2,1)S(1)}, bf16[2,16,320]{2,1,0:T(8,128)(2,1)S(1)}, u32[]{:S(2)}, u32[]{:S(2)}) collective-permute-start(bf16[2,16,320]{2,1,0:T(8,128)(2,1)S(1)} %constant_dynamic-slice_fusion.4), channel_id=1, source_target_pairs={{2,0},{3,1},{4,2},{5,3},{6,4},{7,5},{8,6},{9,7},{10,8},{11,9},{12,... | collective-permute-start | bytes 61448 | tf_op jit(solution)/shard_map/ppermute | solution.py:70
  31.7 11.8 %collective-permute-start.9 = (bf16[32,2048]{1,0:T(8,128)(2,1)S(1)}, bf16[32,2048]{1,0:T(8,128)(2,1)S(1)}, u32[]{:S(2)}, u32[]{:S(2)}) collective-permute-start(bf16[32,2048]{1,0:T(8,128)(2,1)S(1)} %collective-permute-done.7), channel_id=1, source_target_pairs={{0,4},{1,5},{2,6},{3,7},{4,8},{5,9},{6,10},{7,11},{8,12},{9,13},{1... | collective-permute-start | bytes 393224 | tf_op jit(solution)/shard_map/ppermute | solution.py:63
  33.0 13.3 %collective-permute-start.10 = (bf16[32,2048]{1,0:T(8,128)(2,1)S(1)}, bf16[32,2048]{1,0:T(8,128)(2,1)S(1)}, u32[]{:S(2)}, u32[]{:S(2)}) collective-permute-start(bf16[32,2048]{1,0:T(8,128)(2,1)S(1)} %collective-permute-done.8), channel_id=1, source_target_pairs={{0,12},{1,13},{2,14},{3,15},{4,0},{5,1},{6,2},{7,3},{8,4},{9,5},{1... | collective-permute-start | bytes 393224 | tf_op jit(solution)/shard_map/ppermute | solution.py:63
  37.6 13.5 %collective-permute-start.31 = (bf16[64,1024]{1,0:T(8,128)(2,1)S(1)}, bf16[64,1024]{1,0:T(8,128)(2,1)S(1)}, u32[]{:S(2)}, u32[]{:S(2)}) collective-permute-start(bf16[64,1024]{1,0:T(8,128)(2,1)S(1)} %get-tuple-element.57), channel_id=1, source_target_pairs={{0,1},{1,0},{2,3},{3,2},{4,5},{5,4},{6,7},{7,6},{8,9},{9,8},{10,11... | collective-permute-start | bytes 393224 | tf_op jit(solution)/shard_map/ppermute | solution.py:63
  43.5 11.1 %collective-permute-start.3 = (bf16[320,256]{1,0:T(8,128)(2,1)S(1)}, bf16[320,256]{1,0:T(8,128)(2,1)S(1)}, u32[]{:S(2)}, u32[]{:S(2)}) collective-permute-start(bf16[320,256]{1,0:T(8,128)(2,1)S(1)} %collective-permute-done.2.wf_a), channel_id=1, source_target_pairs={{0,2},{1,3},{2,0},{3,1},{4,6},{5,7},{6,4},{7,5},{8,10},{9,11},{10,... | collective-permute-start | bytes 491528 | tf_op jit(solution)/shard_map/ppermute | solution.py:63
  46.4 19.2 %copy-start.3 = (s32[4,64]{1,0:T(4,128)S(1)}, s32[4,64]{1,0:T(4,128)}, u32[]{:S(2)}) copy-start(s32[4,64]{1,0:T(4,128)} %refs_3_.1) | copy-start | bytes 3076
  46.4 31.3 %collective-permute-start.12 = (bf16[4,32,2048]{2,1,0:T(8,128)(2,1)S(1)}, bf16[4,32,2048]{2,1,0:T(8,128)(2,1)S(1)}, u32[]{:S(2)}, u32[]{:S(2)}) collective-permute-start(bf16[4,32,2048]{2,1,0:T(8,128)(2,1)S(1)} %pad_maximum_fusion.refs_8_), channel_id=1, source_target_pairs={{0,192},{1,193},{2,194},{3,195},{4,196},{5,197},{6,198},{7,199},{8... | collective-permute-start | bytes 1572872 | tf_op jit(solution)/shard_map/ppermute | solution.py:63
  49.0 28.8 %collective-permute-start.11 = (bf16[4,32,2048]{2,1,0:T(8,128)(2,1)S(1)}, bf16[4,32,2048]{2,1,0:T(8,128)(2,1)S(1)}, u32[]{:S(2)}, u32[]{:S(2)}) collective-permute-start(bf16[4,32,2048]{2,1,0:T(8,128)(2,1)S(1)} %pad_maximum_fusion.refs_8_), channel_id=1, source_target_pairs={{0,64},{1,65},{2,66},{3,67},{4,68},{5,69},{6,70},{7,71},{8,72},{9,... | collective-permute-start | bytes 1572872 | tf_op jit(solution)/shard_map/ppermute | solution.py:63
  49.1 15.4 %collective-permute-start.5 = (bf16[2,32,512]{2,1,0:T(8,128)(2,1)S(1)}, bf16[2,32,512]{2,1,0:T(8,128)(2,1)S(1)}, u32[]{:S(2)}, u32[]{:S(2)}) collective-permute-start(bf16[2,32,512]{2,1,0:T(8,128)(2,1)S(1)} %constant_dynamic-slice_fusion.3), channel_id=1, source_target_pairs={{0,2},{1,3},{2,4},{3,5},{4,6},{5,7},{6,8},{7,9},{8,10},{9,11},{10,... | collective-permute-start | bytes 196616 | tf_op jit(solution)/shard_map/ppermute | solution.py:70
  51.1 21.9 %collective-permute-start.32 = (bf16[64,1024]{1,0:T(8,128)(2,1)S(1)}, bf16[64,1024]{1,0:T(8,128)(2,1)S(1)}, u32[]{:S(2)}, u32[]{:S(2)}) collective-permute-start(bf16[64,1024]{1,0:T(8,128)(2,1)S(1)} %collective-permute-done.31), channel_id=1, source_target_pairs={{0,12},{1,13},{2,14},{3,15},{4,0},{5,1},{6,2},{7,3},{8,4},{9,5},{1... | collective-permute-start | bytes 393224 | tf_op jit(solution)/shard_map/ppermute | solution.py:63
  54.6 9.9 %collective-permute-start.6 = (bf16[2,32,512]{2,1,0:T(8,128)(2,1)S(1)}, bf16[2,32,512]{2,1,0:T(8,128)(2,1)S(1)}, u32[]{:S(2)}, u32[]{:S(2)}) collective-permute-start(bf16[2,32,512]{2,1,0:T(8,128)(2,1)S(1)} %pad_maximum_fusion.3), channel_id=1, source_target_pairs={{0,2},{1,3},{2,4},{3,5},{4,6},{5,7},{6,8},{7,9},{8,10},{9,11},{10,... | collective-permute-start | bytes 196616 | tf_op jit(solution)/shard_map/ppermute | solution.py:70
  64.5 16.0 %collective-permute-start.33 = (bf16[64,1024]{1,0:T(8,128)(2,1)S(1)}, bf16[64,1024]{1,0:T(8,128)(2,1)S(1)}, u32[]{:S(2)}, u32[]{:S(2)}) collective-permute-start(bf16[64,1024]{1,0:T(8,128)(2,1)S(1)} %collective-permute-done.31), channel_id=1, source_target_pairs={{0,4},{1,5},{2,6},{3,7},{4,8},{5,9},{6,10},{7,11},{8,12},{9,13},{1... | collective-permute-start | bytes 393224 | tf_op jit(solution)/shard_map/ppermute | solution.py:63
  64.6 10.8 %collective-permute-start.21 = (bf16[32,2048]{1,0:T(8,128)(2,1)S(1)}, bf16[32,2048]{1,0:T(8,128)(2,1)S(1)}, u32[]{:S(2)}, u32[]{:S(2)}) collective-permute-start(bf16[32,2048]{1,0:T(8,128)(2,1)S(1)} %get-tuple-element.69), channel_id=1, source_target_pairs={{0,64},{1,65},{2,66},{3,67},{4,68},{5,69},{6,70},{7,71},{8,72},{9,... | collective-permute-start | bytes 393224 | tf_op jit(solution)/shard_map/ppermute | solution.py:63
  65.5 29.7 %copy-start.2 = (f32[1024]{0:T(1024)S(1)}, f32[1024]{0:T(1024)}, u32[]{:S(2)}) copy-start(f32[1024]{0:T(1024)} %param.23) | copy-start | bytes 12292
  73.0 7.6 %collective-permute-start.22 = (bf16[32,2048]{1,0:T(8,128)(2,1)S(1)}, bf16[32,2048]{1,0:T(8,128)(2,1)S(1)}, u32[]{:S(2)}, u32[]{:S(2)}) collective-permute-start(bf16[32,2048]{1,0:T(8,128)(2,1)S(1)} %get-tuple-element.69), channel_id=1, source_target_pairs={{0,192},{1,193},{2,194},{3,195},{4,196},{5,197},{6,198},{7,199},{8... | collective-permute-start | bytes 393224 | tf_op jit(solution)/shard_map/ppermute | solution.py:63
  75.3 7.3 %collective-permute-start.34 = (bf16[64,1024]{1,0:T(8,128)(2,1)S(1)}, bf16[64,1024]{1,0:T(8,128)(2,1)S(1)}, u32[]{:S(2)}, u32[]{:S(2)}) collective-permute-start(bf16[64,1024]{1,0:T(8,128)(2,1)S(1)} %collective-permute-done.32), channel_id=1, source_target_pairs={{0,12},{1,13},{2,14},{3,15},{4,0},{5,1},{6,2},{7,3},{8,4},{9,5},{1... | collective-permute-start | bytes 393224 | tf_op jit(solution)/shard_map/ppermute | solution.py:63
  77.7 5.0 %collective-permute-start.23 = (bf16[32,2048]{1,0:T(8,128)(2,1)S(1)}, bf16[32,2048]{1,0:T(8,128)(2,1)S(1)}, u32[]{:S(2)}, u32[]{:S(2)}) collective-permute-start(bf16[32,2048]{1,0:T(8,128)(2,1)S(1)} %collective-permute-done.21), channel_id=1, source_target_pairs={{0,64},{1,65},{2,66},{3,67},{4,68},{5,69},{6,70},{7,71},{8,72},{9,... | collective-permute-start | bytes 393224 | tf_op jit(solution)/shard_map/ppermute | solution.py:63
  77.8 7.8 %collective-permute-start.14 = (bf16[2,32,2048]{2,1,0:T(8,128)(2,1)S(1)}, bf16[2,32,2048]{2,1,0:T(8,128)(2,1)S(1)}, u32[]{:S(2)}, u32[]{:S(2)}) collective-permute-start(bf16[2,32,2048]{2,1,0:T(8,128)(2,1)S(1)} %slice.30), channel_id=1, source_target_pairs={{0,192},{1,193},{2,194},{3,195},{4,196},{5,197},{6,198},{7,199},{8... | collective-permute-start | bytes 786440 | tf_op jit(solution)/shard_map/ppermute | solution.py:63
  80.5 7.9 %collective-permute-start.13 = (bf16[2,32,2048]{2,1,0:T(8,128)(2,1)S(1)}, bf16[2,32,2048]{2,1,0:T(8,128)(2,1)S(1)}, u32[]{:S(2)}, u32[]{:S(2)}) collective-permute-start(bf16[2,32,2048]{2,1,0:T(8,128)(2,1)S(1)} %slice.29), channel_id=1, source_target_pairs={{0,64},{1,65},{2,66},{3,67},{4,68},{5,69},{6,70},{7,71},{8,72},{9,... | collective-permute-start | bytes 786440 | tf_op jit(solution)/shard_map/ppermute | solution.py:63
  80.6 10.4 %collective-permute-start.15 = (bf16[4,32,2048]{2,1,0:T(8,128)(2,1)S(1)}, bf16[4,32,2048]{2,1,0:T(8,128)(2,1)S(1)}, u32[]{:S(2)}, u32[]{:S(2)}) collective-permute-start(bf16[4,32,2048]{2,1,0:T(8,128)(2,1)S(1)} %pad_maximum_fusion.refs_8_), channel_id=1, source_target_pairs={{0,2},{1,3},{2,0},{3,1},{4,6},{5,7},{6,4},{7,5},{8,10},{9,11},{10,... | collective-permute-start | bytes 1572872 | tf_op jit(solution)/shard_map/ppermute | solution.py:63
  82.6 11.1 %collective-permute-start.17 = (bf16[4,32,2048]{2,1,0:T(8,128)(2,1)S(1)}, bf16[4,32,2048]{2,1,0:T(8,128)(2,1)S(1)}, u32[]{:S(2)}, u32[]{:S(2)}) collective-permute-start(bf16[4,32,2048]{2,1,0:T(8,128)(2,1)S(1)} %collective-permute-done.12.refs_10_), channel_id=1, source_target_pairs={{0,2},{1,3},{2,0},{3,1},{4,6},{5,7},{6,4},{7,5},{8,10},{9,11},{10,... | collective-permute-start | bytes 1572872 | tf_op jit(solution)/shard_map/ppermute | solution.py:63
  82.8 12.5 %collective-permute-start.16 = (bf16[4,32,2048]{2,1,0:T(8,128)(2,1)S(1)}, bf16[4,32,2048]{2,1,0:T(8,128)(2,1)S(1)}, u32[]{:S(2)}, u32[]{:S(2)}) collective-permute-start(bf16[4,32,2048]{2,1,0:T(8,128)(2,1)S(1)} %collective-permute-done.11.refs_9_), channel_id=1, source_target_pairs={{0,2},{1,3},{2,0},{3,1},{4,6},{5,7},{6,4},{7,5},{8,10},{9,11},{10,... | collective-permute-start | bytes 1572872 | tf_op jit(solution)/shard_map/ppermute | solution.py:63
  85.6 5.6 %collective-permute-start.19 = (bf16[2,32,2048]{2,1,0:T(8,128)(2,1)S(1)}, bf16[2,32,2048]{2,1,0:T(8,128)(2,1)S(1)}, u32[]{:S(2)}, u32[]{:S(2)}) collective-permute-start(bf16[2,32,2048]{2,1,0:T(8,128)(2,1)S(1)} %collective-permute-done.14.refs_12_), channel_id=1, source_target_pairs={{0,2},{1,3},{2,0},{3,1},{4,6},{5,7},{6,4},{7,5},{8,10},{9,11},{10,... | collective-permute-start | bytes 786440 | tf_op jit(solution)/shard_map/ppermute | solution.py:63
  88.4 5.7 %collective-permute-start.18 = (bf16[2,32,2048]{2,1,0:T(8,128)(2,1)S(1)}, bf16[2,32,2048]{2,1,0:T(8,128)(2,1)S(1)}, u32[]{:S(2)}, u32[]{:S(2)}) collective-permute-start(bf16[2,32,2048]{2,1,0:T(8,128)(2,1)S(1)} %collective-permute-done.13.refs_11_), channel_id=1, source_target_pairs={{0,2},{1,3},{2,0},{3,1},{4,6},{5,7},{6,4},{7,5},{8,10},{9,11},{10,... | collective-permute-start | bytes 786440 | tf_op jit(solution)/shard_map/ppermute | solution.py:63
  91.0 19.0 %collective-permute-start.35 = (bf16[4,64,1024]{2,1,0:T(8,128)(2,1)S(1)}, bf16[4,64,1024]{2,1,0:T(8,128)(2,1)}, u32[]{:S(2)}, u32[]{:S(2)}) collective-permute-start(bf16[4,64,1024]{2,1,0:T(8,128)(2,1)S(1)} %pad_maximum_fusion.2.refs_12_), channel_id=1, source_target_pairs={{0,64},{1,65},{2,66},{3,67},{4,68},{5,69},{6,70},{7,71},{8,72},{9,... | collective-permute-start | bytes 1572872 | tf_op jit(solution)/shard_map/ppermute | solution.py:63
  91.1 20.6 %collective-permute-start.36 = (bf16[4,64,1024]{2,1,0:T(8,128)(2,1)S(1)}, bf16[4,64,1024]{2,1,0:T(8,128)(2,1)}, u32[]{:S(2)}, u32[]{:S(2)}) collective-permute-start(bf16[4,64,1024]{2,1,0:T(8,128)(2,1)S(1)} %pad_maximum_fusion.2.refs_12_), channel_id=1, source_target_pairs={{0,192},{1,193},{2,194},{3,195},{4,196},{5,197},{6,198},{7,199},{8... | collective-permute-start | bytes 1572872 | tf_op jit(solution)/shard_map/ppermute | solution.py:63
  93.8 16.3 %collective-permute-start.24 = (bf16[4,32,2048]{2,1,0:T(8,128)(2,1)S(1)}, bf16[4,32,2048]{2,1,0:T(8,128)(2,1)S(1)}, u32[]{:S(2)}, u32[]{:S(2)}) collective-permute-start(bf16[4,32,2048]{2,1,0:T(8,128)(2,1)S(1)} %pad_maximum_fusion.1.refs_4_), channel_id=1, source_target_pairs={{0,12},{1,13},{2,14},{3,15},{4,0},{5,1},{6,2},{7,3},{8,4},{9,5},{1... | collective-permute-start | bytes 1572872 | tf_op jit(solution)/shard_map/ppermute | solution.py:63
  94.1 19.0 %collective-permute-start.25 = (bf16[4,32,2048]{2,1,0:T(8,128)(2,1)S(1)}, bf16[4,32,2048]{2,1,0:T(8,128)(2,1)S(1)}, u32[]{:S(2)}, u32[]{:S(2)}) collective-permute-start(bf16[4,32,2048]{2,1,0:T(8,128)(2,1)S(1)} %pad_maximum_fusion.1.refs_4_), channel_id=1, source_target_pairs={{0,4},{1,5},{2,6},{3,7},{4,8},{5,9},{6,10},{7,11},{8,12},{9,13},{1... | collective-permute-start | bytes 1572872 | tf_op jit(solution)/shard_map/ppermute | solution.py:63
  110.0 14.0 %collective-permute-start.37 = (bf16[4,64,1024]{2,1,0:T(8,128)(2,1)}, bf16[4,64,1024]{2,1,0:T(8,128)(2,1)}, u32[]{:S(2)}, u32[]{:S(2)}) collective-permute-start(bf16[4,64,1024]{2,1,0:T(8,128)(2,1)} %collective-permute-done.35.refs_13_), channel_id=1, source_target_pairs={{0,64},{1,65},{2,66},{3,67},{4,68},{5,69},{6,70},{7,71},{8,72},{9,... | collective-permute-start | bytes 1572872 | tf_op jit(solution)/shard_map/ppermute | solution.py:63
  110.1 27.4 %collective-permute-start.26 = (bf16[4,32,2048]{2,1,0:T(8,128)(2,1)S(1)}, bf16[4,32,2048]{2,1,0:T(8,128)(2,1)S(1)}, u32[]{:S(2)}, u32[]{:S(2)}) collective-permute-start(bf16[4,32,2048]{2,1,0:T(8,128)(2,1)S(1)} %collective-permute-done.24.refs_5_), channel_id=1, source_target_pairs={{0,12},{1,13},{2,14},{3,15},{4,0},{5,1},{6,2},{7,3},{8,4},{9,5},{1... | collective-permute-start | bytes 1572872 | tf_op jit(solution)/shard_map/ppermute | solution.py:63
  111.7 28.2 %collective-permute-start.40 = (bf16[4,64,1024]{2,1,0:T(8,128)(2,1)}, bf16[4,64,1024]{2,1,0:T(8,128)(2,1)}, u32[]{:S(2)}, u32[]{:S(2)}) collective-permute-start(bf16[4,64,1024]{2,1,0:T(8,128)(2,1)} %collective-permute-done.36.refs_14_), channel_id=1, source_target_pairs={{0,2},{1,3},{2,0},{3,1},{4,6},{5,7},{6,4},{7,5},{8,10},{9,11},{10,... | collective-permute-start | bytes 1572872 | tf_op jit(solution)/shard_map/ppermute | solution.py:63
  113.1 27.2 %collective-permute-start.39 = (bf16[4,64,1024]{2,1,0:T(8,128)(2,1)}, bf16[4,64,1024]{2,1,0:T(8,128)(2,1)}, u32[]{:S(2)}, u32[]{:S(2)}) collective-permute-start(bf16[4,64,1024]{2,1,0:T(8,128)(2,1)} %collective-permute-done.35.refs_13_), channel_id=1, source_target_pairs={{0,2},{1,3},{2,0},{3,1},{4,6},{5,7},{6,4},{7,5},{8,10},{9,11},{10,... | collective-permute-start | bytes 1572872 | tf_op jit(solution)/shard_map/ppermute | solution.py:63
  113.1 27.3 %collective-permute-start.38 = (bf16[4,64,1024]{2,1,0:T(8,128)(2,1)S(1)}, bf16[4,64,1024]{2,1,0:T(8,128)(2,1)}, u32[]{:S(2)}, u32[]{:S(2)}) collective-permute-start(bf16[4,64,1024]{2,1,0:T(8,128)(2,1)S(1)} %pad_maximum_fusion.2.refs_12_), channel_id=1, source_target_pairs={{0,2},{1,3},{2,0},{3,1},{4,6},{5,7},{6,4},{7,5},{8,10},{9,11},{10,... | collective-permute-start | bytes 1572872 | tf_op jit(solution)/shard_map/ppermute | solution.py:63
  124.0 15.8 %collective-permute-start.20 = (bf16[2,64,512]{2,1,0:T(8,128)(2,1)S(1)}, bf16[2,64,512]{2,1,0:T(8,128)(2,1)S(1)}, u32[]{:S(2)}, u32[]{:S(2)}) collective-permute-start(bf16[2,64,512]{2,1,0:T(8,128)(2,1)S(1)} %get-tuple-element.67), channel_id=1, source_target_pairs={{0,1},{1,0},{2,3},{3,2},{4,5},{5,4},{6,7},{7,6},{8,9},{9,8},{10,11... | collective-permute-start | bytes 393224 | tf_op jit(solution)/shard_map/ppermute | solution.py:63
  137.5 4.6 %collective-permute-start.28 = (bf16[4,32,2048]{2,1,0:T(8,128)(2,1)S(1)}, bf16[4,32,2048]{2,1,0:T(8,128)(2,1)S(1)}, u32[]{:S(2)}, u32[]{:S(2)}) collective-permute-start(bf16[4,32,2048]{2,1,0:T(8,128)(2,1)S(1)} %collective-permute-done.24.refs_5_), channel_id=1, source_target_pairs={{0,2},{1,3},{2,0},{3,1},{4,6},{5,7},{6,4},{7,5},{8,10},{9,11},{10,... | collective-permute-start | bytes 1572872 | tf_op jit(solution)/shard_map/ppermute | solution.py:63
  139.8 2.3 %collective-permute-start.29 = (bf16[4,32,2048]{2,1,0:T(8,128)(2,1)S(1)}, bf16[4,32,2048]{2,1,0:T(8,128)(2,1)S(1)}, u32[]{:S(2)}, u32[]{:S(2)}) collective-permute-start(bf16[4,32,2048]{2,1,0:T(8,128)(2,1)S(1)} %collective-permute-done.25.refs_6_), channel_id=1, source_target_pairs={{0,2},{1,3},{2,0},{3,1},{4,6},{5,7},{6,4},{7,5},{8,10},{9,11},{10,... | collective-permute-start | bytes 1572872 | tf_op jit(solution)/shard_map/ppermute | solution.py:63
  139.9 2.9 %collective-permute-start.27 = (bf16[4,32,2048]{2,1,0:T(8,128)(2,1)S(1)}, bf16[4,32,2048]{2,1,0:T(8,128)(2,1)S(1)}, u32[]{:S(2)}, u32[]{:S(2)}) collective-permute-start(bf16[4,32,2048]{2,1,0:T(8,128)(2,1)S(1)} %pad_maximum_fusion.1.refs_4_), channel_id=1, source_target_pairs={{0,2},{1,3},{2,0},{3,1},{4,6},{5,7},{6,4},{7,5},{8,10},{9,11},{10,... | collective-permute-start | bytes 1572872 | tf_op jit(solution)/shard_map/ppermute | solution.py:63
  140.3 3.3 %collective-permute-start.41 = (bf16[4,64,1024]{2,1,0:T(8,128)(2,1)}, bf16[4,64,1024]{2,1,0:T(8,128)(2,1)S(1)}, u32[]{:S(2)}, u32[]{:S(2)}) collective-permute-start(bf16[4,64,1024]{2,1,0:T(8,128)(2,1)} %collective-permute-done.37.refs_15_), channel_id=1, source_target_pairs={{0,2},{1,3},{2,0},{3,1},{4,6},{5,7},{6,4},{7,5},{8,10},{9,11},{10,... | collective-permute-start | bytes 1572872 | tf_op jit(solution)/shard_map/ppermute | solution.py:63
  140.4 3.9 %collective-permute-start.30 = (bf16[4,32,2048]{2,1,0:T(8,128)(2,1)S(1)}, bf16[4,32,2048]{2,1,0:T(8,128)(2,1)S(1)}, u32[]{:S(2)}, u32[]{:S(2)}) collective-permute-start(bf16[4,32,2048]{2,1,0:T(8,128)(2,1)S(1)} %collective-permute-done.26.refs_7_), channel_id=1, source_target_pairs={{0,2},{1,3},{2,0},{3,1},{4,6},{5,7},{6,4},{7,5},{8,10},{9,11},{10,... | collective-permute-start | bytes 1572872 | tf_op jit(solution)/shard_map/ppermute | solution.py:63
  143.6 0.8 copy-start.5
  158.4 29.1 %collective-permute-start.42 = (bf16[2,256,512]{2,1,0:T(8,128)(2,1)}, bf16[2,256,512]{2,1,0:T(8,128)(2,1)S(1)}, u32[]{:S(2)}, u32[]{:S(2)}) collective-permute-start(bf16[2,256,512]{2,1,0:T(8,128)(2,1)} %get-tuple-element.64), channel_id=1, source_target_pairs={{0,1},{1,0},{2,3},{3,2},{4,5},{5,4},{6,7},{7,6},{8,9},{9,8},{10,11... | collective-permute-start | bytes 1572872 | tf_op jit(solution)/shard_map/ppermute | solution.py:63
